TPU v7x, 256 devices: a whole 4x4x8 slice. The times are simulated.
256 devices in a mesh: rows: 128 (over z, y, x), cols: 2 (over core).
Axes of the slice: x: 4, y: 4, z: 8, core: 2. Of those that a mesh axis runs over, the one named last changes fastest.
Arguments:
- design: float32 [131072, 512], P('rows', 'cols'), may hold values from -24 to 24
- signs: int32 [131072], P('rows'), may hold values from -1 to 1, as said below
- kept: int32 [8192], replicated, may hold values from 0 to 131071, as said below
Outputs:
- sketch: float32 [8192, 512], P('rows', 'cols')
- factor: float32 [512, 512], P(None, 'cols')
Inputs may be any that keep to these rules, and one draw needn't show every extreme that they name: `signs`: each entry is +1 or -1. `kept`: distinct and increasing.
All inputs are finite; a program needn't handle non-finite values.
Results may differ from a plain program's by a relative error of at most 0.0003.
Values sent between devices are 32-bit elements; how exact they have to be, the bound alone decides.
No kernel may reach another device: no remote copies, remote signals or barrier semaphores. Data moves between devices by JAX's collectives and lax.ppermute only.
A program may use at most 64 MiB of HBM per device.

v0:
```python
import math

import jax
import jax.numpy as jnp
from jax import lax
from jax.sharding import Mesh
from jax.sharding import PartitionSpec as P

ROWS = ("rows_0", "rows_1", "rows_2")


def sum_by_axis(so_far, axes):
    for axis in axes:
        so_far = lax.psum_scatter(so_far, axis, scatter_dimension=0, tiled=True)
    return so_far


def laid_out(parts, dim):
    dims = list(parts.shape[1:])
    dims[dim] *= parts.shape[0]
    return jnp.moveaxis(parts, 0, dim).reshape(dims)


def copy_for_each(shard, axis):
    length = lax.axis_size(axis)
    return lax.all_to_all(
        jnp.broadcast_to(shard[None], (length, *shard.shape)), axis, 0, 0, tiled=True
    )


def gathered_copies(shard, axis, dim):
    return laid_out(copy_for_each(shard, axis), dim)


def hadamard(order):
    matrix = jnp.ones((1, 1), jnp.float32)
    base = jnp.array([[1.0, 1.0], [1.0, -1.0]], jnp.float32)
    while matrix.shape[0] < order:
        matrix = jnp.kron(matrix, base)
    return matrix


def bit_parity(value):
    folded = value
    for amount in (16, 8, 4, 2, 1):
        folded = jnp.bitwise_xor(folded, jnp.right_shift(folded, amount))
    return jnp.bitwise_and(folded, 1)


def local_transform(flipped):
    length, width = flipped.shape
    outer = length // 128
    inner_table = hadamard(128)
    outer_table = hadamard(outer)
    blocks = flipped.reshape(outer, 128, width)
    mixed = jnp.einsum("pb,abc->apc", inner_table, blocks, precision=lax.Precision.HIGHEST)
    mixed = jnp.einsum("qa,apc->qpc", outer_table, mixed, precision=lax.Precision.HIGHEST)
    return mixed.reshape(length, width)


def signed_rows(transformed, kept_part, device_row, total_rows):
    length = transformed.shape[0]
    kept_blocks = kept_part // length
    offsets = kept_part - kept_blocks * length
    parity = bit_parity(jnp.bitwise_and(kept_blocks, device_row))
    factor = (1.0 - 2.0 * parity.astype(jnp.float32)) / math.sqrt(total_rows)
    return jnp.take(transformed, offsets, axis=0) * factor[:, None]


def body(design, signs, kept):
    flipped = design * signs.astype(jnp.float32)[:, None]
    transformed = local_transform(flipped)
    device_row = lax.axis_index(ROWS)
    groups = lax.axis_size(ROWS)
    length = transformed.shape[0]
    widths = transformed.shape[1]
    total_rows = length * groups
    sketch = sum_by_axis(signed_rows(transformed, kept, device_row, total_rows), ROWS)
    column = lax.axis_index("cols")
    whole = gathered_copies(sketch, "cols", 1)
    kept_total = kept.shape[0]
    partial_gram = jnp.dot(
        whole.T, whole, precision=lax.Precision.HIGHEST, preferred_element_type=jnp.float32
    )
    gram = lax.psum(partial_gram, ROWS) / kept_total
    factor = jnp.linalg.cholesky(gram).T
    return (sketch, lax.dynamic_slice_in_dim(factor, column * widths, widths, 1))


def solution(mesh):
    torus = Mesh(
        mesh.devices.reshape(8, 4, 4, mesh.shape["cols"]), ("rows_0", "rows_1", "rows_2", "cols")
    )
    return jax.shard_map(
        body,
        mesh=torus,
        in_specs=(P(ROWS, "cols"), P(ROWS), P()),
        out_specs=(P(ROWS, "cols"), P(None, "cols")),
        check_vma=False,
    )
```

profile of v0, /device:TPU:1, one launch (start us, length us, event | category | flops | bytes accessed | tf_op | source)
XLA Modules:
  0.0 536.3 jit_solution(2784497924892284188)
XLA Ops:
  7.2 0.8 broadcast_multiply_fusion.7
  13.1 0.9 broadcast_multiply_fusion.2
  14.7 3.0 broadcast_multiply_fusion
  17.7 4.0 reshape.195
  21.9 1.8 convolution_bitcast_fusion
  24.2 1.0 fusion.21
  25.6 31.4 %gather_fusion = f32[8192,256]{1,0:T(8,128)} fusion(f32[1024,256]{1,0:T(8,128)S(1)} %bitcast.45, s32[8192]{0:T(1024)S(1)} %broadcast_clamp_fusion), kind=kCustom, calls=%fused_computation | custom fusion | bytes 16809984 | tf_op jit(solution)/shard_map/jit(_take)/gather | solution.py:67
  57.0 9.9 %select_multiply_fusion = f32[8192,256]{1,0:T(8,128)} fusion(f32[8192,256]{1,0:T(8,128)} %gather_fusion, f32[8192]{0:T(1024)S(1)} %fusion.19, pred[8192]{0:T(1024)(128)(4,1)S(1)} %compare_and_fusion), kind=kLoop, calls=%fused_computation.1 | loop fusion | flops 4194304 | bytes 16818176 | tf_op jit(solution)/shard_map/mul | solution.py:67
  66.9 98.9 %reduce-scatter.4.cloned.1.call-done = f32[1024,256]{1,0:T(8,128)} async-done(((f32[8192,256]{1,0:T(8,128)}), f32[1024,256]{1,0:T(8,128)}) %reduce-scatter.4.cloned.1.call-update) | async-done | bytes 1048592 | tf_op jit(solution)/shard_map/reduce_scatter | solution.py:14
  165.9 25.8 %reduce-scatter.6.cloned.1.call-done = f32[256,256]{1,0:T(8,128)} async-done(((f32[1024,256]{1,0:T(8,128)}), f32[256,256]{1,0:T(8,128)}) %reduce-scatter.6.cloned.1.call-update) | async-done | bytes 262160 | tf_op jit(solution)/shard_map/reduce_scatter | solution.py:14
  191.7 25.3 %reduce-scatter.8.cloned.1.call-done = f32[64,256]{1,0:T(8,128)} async-done(((f32[256,256]{1,0:T(8,128)}), f32[64,256]{1,0:T(8,128)}) %reduce-scatter.8.cloned.1.call-update) | async-done | bytes 65552 | tf_op jit(solution)/shard_map/reduce_scatter | solution.py:14
  217.9 6.4 %all_to_all.5 = f32[2,64,256]{2,1,0:T(8,128)S(1)} all-to-all(f32[2,64,256]{2,1,0:T(8,128)S(1)} %broadcast_in_dim.59), channel_id=1, replica_groups=mesh['rows_0'=8,'rows_1'=4,'rows_2'=4,'cols'=2] {'cols'}, dimensions={0} | all-to-all | bytes 262144 | tf_op jit(solution)/shard_map/all_to_all | solution.py:26
  224.3 2.1 fusion.22
  226.4 216.0 %all-reduce.3.cloned.1.call-done = f32[512,512]{0,1:T(8,128)} async-done(((f32[512,512]{0,1:T(8,128)}), f32[512,512]{0,1:T(8,128)}) %all-reduce.3.cloned.1.call-update) | async-done | bytes 1048592 | tf_op jit(solution)/shard_map/psum | solution.py:85
  442.3 1.3 broadcast_multiply_fusion.1
  444.0 1.5 fusion
  445.5 11.7 %cholesky.104 = f32[128,128]{1,0:T(8,128)S(1)} custom-call(f32[128,128]{1,0:T(8,128)S(1)} %cholesky.266), custom_call_target="Cholesky" | custom-call | tf_op jit(solution)/shard_map/jit(cholesky)/cholesky | solution.py:86
  457.4 9.8 %custom-call.27 = f32[1,128,128]{1,2,0:T(8,128)S(1)} custom-call(f32[1,128,128]{2,1,0:T(8,128)S(1)} %get-tuple-element.17), custom_call_target="InvertDiagBlocksLowerTriangular" | custom-call | tf_op jit(solution)/shard_map/jit(cholesky)/cholesky | solution.py:86
  467.8 11.7 %cholesky.217 = f32[128,128]{1,0:T(8,128)S(1)} custom-call(f32[128,128]{1,0:T(8,128)S(1)} %cholesky.270), custom_call_target="Cholesky" | custom-call | tf_op jit(solution)/shard_map/jit(cholesky)/cholesky | solution.py:86
  479.6 9.9 %custom-call.28 = f32[1,128,128]{1,2,0:T(8,128)S(1)} custom-call(f32[1,128,128]{2,1,0:T(8,128)S(1)} %get-tuple-element.14), custom_call_target="InvertDiagBlocksLowerTriangular" | custom-call | tf_op jit(solution)/shard_map/jit(cholesky)/cholesky | solution.py:86
  490.2 11.7 %cholesky.238 = f32[128,128]{1,0:T(8,128)S(1)} custom-call(f32[128,128]{1,0:T(8,128)S(1)} %cholesky.275), custom_call_target="Cholesky" | custom-call | tf_op jit(solution)/shard_map/jit(cholesky)/cholesky | solution.py:86
  502.0 9.8 %custom-call.29 = f32[1,128,128]{1,2,0:T(8,128)S(1)} custom-call(f32[1,128,128]{2,1,0:T(8,128)S(1)} %get-tuple-element.11), custom_call_target="InvertDiagBlocksLowerTriangular" | custom-call | tf_op jit(solution)/shard_map/jit(cholesky)/cholesky | solution.py:86
  512.4 11.7 %cholesky.255 = f32[128,128]{1,0:T(8,128)S(1)} custom-call(f32[128,128]{1,0:T(8,128)S(1)} %convolution_subtract_fusion.2), custom_call_target="Cholesky" | custom-call | tf_op jit(solution)/shard_map/jit(cholesky)/cholesky | solution.py:86
  528.8 1.0 copy.20
  (49 shorter events, 12.4 us)
Async XLA Ops:
  7.2 14.5 %copy-start = (f32[1024,256]{1,0:T(8,128)S(1)}, f32[1024,256]{1,0:T(8,128)}, u32[]{:S(2)}) copy-start(f32[1024,256]{1,0:T(8,128)} %param.5) | copy-start | bytes 3145732
  7.2 158.6 %reduce-scatter.4.cloned.1.call-start = ((), (), s32[]{:S(2)}) async-start(), calls=%async_computation.4 | async-start | bytes 9437184 | tf_op jit(solution)/shard_map/reduce_scatter | solution.py:14
  17.7 7.9 %copy-start.1 = (s32[8192]{0:T(1024)S(1)}, s32[8192]{0:T(1024)}, u32[]{:S(2)}) copy-start(s32[8192]{0:T(1024)} %param.7) | copy-start | bytes 98308
  66.9 124.8 %reduce-scatter.6.cloned.1.call-start = ((), (), s32[]{:S(2)}) async-start(), calls=%async_computation.5 | async-start | bytes 1310720 | tf_op jit(solution)/shard_map/reduce_scatter | solution.py:14
  165.8 51.2 %reduce-scatter.8.cloned.1.call-start = ((), (), s32[]{:S(2)}) async-start(), calls=%async_computation.6 | async-start | bytes 327680 | tf_op jit(solution)/shard_map/reduce_scatter | solution.py:14
  191.7 250.6 %all-reduce.3.cloned.1.call-start = ((), (), s32[]{:S(2)}) async-start(), calls=%async_computation.7 | async-start | bytes 2097152 | tf_op jit(solution)/shard_map/psum | solution.py:85
Sparse Core Ops, SparseCore 0:
  67.0 98.7 reduce-scatter.3
  168.4 23.2 reduce-scatter.5
  194.9 22.0 reduce-scatter.7
  226.5 215.8 all-reduce.2
where the time goes:
time: 541 us; the launch traced here: 536 us
  waiting for transfers between devices  366 us (68%)
  other arithmetic  101 us (19%)
  local copies, waits for them, and re-layouts  39.6 us (7%)
  between operations  16.6 us (3%)
  matrix products  6.71 us (1%)
  blocking collectives  6.39 us (1%)
    psum x1, waiting for transfers between devices, body(): gram = lax.psum(partial_gram, ROWS) / kept_total  216 us
    reduce_scatter x3, waiting for transfers between devices, sum_by_axis(): so_far = lax.psum_scatter(so_far, axis, scatter_dimension=0, tiled=True)  150 us
    another operation x14, other arithmetic, body(): factor = jnp.linalg.cholesky(gram).T  78.6 us
    gather x1, local copies, waits for them, and re-layouts, signed_rows(): return jnp.take(transformed, offsets, axis=0) * factor[:, None]  31.4 us
  transfers between devices with their start and end apart: 4, of which 4 were waited for; matrix products, arithmetic and copies ran while one was open for 0% of the time, Pallas kernels for 0%

commit v1 on v0

v1 whole, which is shorter than its diff:
```python
import functools
import math

import jax
import jax.numpy as jnp
from jax import lax
from jax.experimental import pallas as pl
from jax.experimental.pallas import tpu as pltpu
from jax.sharding import Mesh
from jax.sharding import PartitionSpec as P

ROWS = ("rows_0", "rows_1", "rows_2")
PLANE = ("rows_1", "rows_2")
VMEM = pl.BlockSpec(memory_space=pltpu.VMEM)
SMEM = pl.BlockSpec(memory_space=pltpu.SMEM)
LIMIT = pltpu.CompilerParams(vmem_limit_bytes=32 * 1024 * 1024)
WINDOW = 4


def butterflies(values):
    values = list(values)
    half = 1
    while half < len(values):
        for low in range(len(values)):
            if not low & half:
                a, b = values[low], values[low | half]
                values[low], values[low | half] = a + b, a - b
        half *= 2
    return values


def sylvester(order):
    parity = lax.broadcasted_iota(jnp.int32, (order, order), 0)
    parity = parity & lax.broadcasted_iota(jnp.int32, (order, order), 1)
    for amount in (4, 2, 1):
        parity = parity ^ (parity >> amount)
    return (1 - 2 * (parity & 1)).astype(jnp.float32).astype(jnp.bfloat16)


def local_kernel(design_ref, signs_ref, out_ref):
    table = sylvester(128)
    for half in range(2):
        parts = []
        for b in range(8):
            piece = design_ref[b * 128 : (b + 1) * 128, half * 128 : (half + 1) * 128].T
            piece = piece * signs_ref[b : b + 1, :].astype(jnp.float32)
            high = piece.astype(jnp.bfloat16)
            rest = piece - high.astype(jnp.float32)
            middle = rest.astype(jnp.bfloat16)
            low = (rest - middle.astype(jnp.float32)).astype(jnp.bfloat16)
            total = jnp.dot(low, table, preferred_element_type=jnp.float32)
            total += jnp.dot(middle, table, preferred_element_type=jnp.float32)
            total += jnp.dot(high, table, preferred_element_type=jnp.float32)
            parts.append(total)
        for q, mixed in enumerate(butterflies(parts)):
            out_ref[pl.ds(half * 8 + q, 128, stride=16), :] = mixed


def select_kernel(scale, columns_ref, kept_ref, kept_scalar_ref, out_ref, work, first, second):
    for low in range(16):
        mixed = butterflies(columns_ref[high * 16 + low] for high in range(8))
        for high in range(8):
            work[high * 16 + low] = mixed[high]
    for high in range(8):
        mixed = butterflies(work[high * 16 + low] for low in range(16))
        for low in range(16):
            work[high * 16 + low] = mixed[low]
    sublane = lax.broadcasted_iota(jnp.int32, (8, 128), 0)

    def picked(block, lane, key, so_far):
        found = key == sublane + block * 8
        return tuple(
            jnp.where(found, jnp.take_along_axis(work[block, h * 8 : h * 8 + 8, :], lane, axis=1), so_far[h])
            for h in range(2)
        )

    def ids(chunk):
        wanted = jnp.broadcast_to(kept_ref[pl.ds(chunk, 1), :], (8, 128))
        return wanted & 127, wanted >> 7

    zero = jnp.zeros((8, 128), jnp.float32)

    def group(step, carry):
        for inner in range(8):
            chunk = step * 8 + inner
            start = kept_scalar_ref[chunk * 128] >> 10
            lane, key = ids(chunk)
            so_far = (zero, zero)
            for w in range(WINDOW):
                so_far = picked(jnp.minimum(start + w, 127), lane, key, so_far)
            first[pl.ds(chunk, 1), :] = jnp.sum(so_far[0], axis=0, keepdims=True)
            second[pl.ds(chunk, 1), :] = jnp.sum(so_far[1], axis=0, keepdims=True)
        return carry

    lax.fori_loop(0, 8, group, 0)

    def rest(chunk, carry):
        start = (kept_scalar_ref[chunk * 128] >> 10) + WINDOW
        stop = (kept_scalar_ref[chunk * 128 + 127] >> 10) + 1

        @pl.when(stop > start)
        def _():
            lane, key = ids(chunk)
            more = lax.fori_loop(start, stop, lambda block, c: picked(block, lane, key, c), (zero, zero))
            first[pl.ds(chunk, 1), :] += jnp.sum(more[0], axis=0, keepdims=True)
            second[pl.ds(chunk, 1), :] += jnp.sum(more[1], axis=0, keepdims=True)

        return carry

    lax.fori_loop(0, 64, rest, 0)
    left = lax.broadcasted_iota(jnp.int32, (64, 128), 1) < 64
    a, b = first[...] * scale, second[...] * scale
    out_ref[pl.ds(0, 64, stride=2), :] = jnp.where(left, a, pltpu.roll(b, 64, 1))
    out_ref[pl.ds(1, 64, stride=2), :] = jnp.where(left, pltpu.roll(a, 64, 1), b)


def turn_kernel(entries_ref, sketch_ref):
    turned = entries_ref[...].T
    sketch_ref[:, :128] = turned[:64]
    sketch_ref[:, 128:] = turned[64:]


def gram_kernel(scale, column_ref, own_ref, other_ref, out_ref):
    own = [own_ref[:, :128], own_ref[:, 128:]]
    other = [other_ref[:, :128], other_ref[:, 128:]]
    zero = column_ref[0] == 0

    def choose(a, b):
        return jnp.where(zero, a, b)

    left = choose(own[0], other[1])
    pairs = [
        (own[0], own[0]),
        (own[0], own[1]),
        (own[1], own[1]),
        (left, choose(other[0], own[0])),
        (left, choose(other[1], own[1])),
    ]
    for index, (a, b) in enumerate(pairs):
        out_ref[index * 128 : (index + 1) * 128, :] = scale * lax.dot_general(
            a, b, (((0,), (0,)), ((), ())), precision=lax.Precision.HIGHEST, preferred_element_type=jnp.float32
        )


def copies(shard, axes, count):
    return lax.all_to_all(jnp.broadcast_to(shard[None], (count, *shard.shape)), axes, 0, 0, tiled=True)


def swap_cores(value):
    return lax.ppermute(value, "cols", [(0, 1), (1, 0)])


def whole_gram(first, second):
    b = [first[i * 128 : (i + 1) * 128] for i in range(5)]
    d = [second[i * 128 : (i + 1) * 128] for i in range(5)]
    rows = [
        [b[0], b[1], b[3], b[4]],
        [b[1].T, b[2], d[3], d[4]],
        [b[3].T, d[3].T, d[0], d[1]],
        [b[4].T, d[4].T, d[1].T, d[2]],
    ]
    return jnp.concatenate([jnp.concatenate(r, 1) for r in rows], 0)


def body(design, signs, kept):
    f32 = jnp.float32
    column = lax.axis_index("cols")
    local = pl.pallas_call(
        local_kernel,
        out_shape=jax.ShapeDtypeStruct((2048, 128), f32),
        in_specs=[VMEM, VMEM],
        out_specs=VMEM,
        compiler_params=LIMIT,
        name="local_transform",
    )(design, signs.reshape(8, 128))
    columns = lax.all_to_all(local.reshape(128, 16, 128), ROWS, 0, 0, tiled=True)
    entries = pl.pallas_call(
        functools.partial(select_kernel, 1.0 / math.sqrt(131072)),
        out_shape=jax.ShapeDtypeStruct((128, 128), f32),
        in_specs=[VMEM, VMEM, SMEM],
        out_specs=VMEM,
        scratch_shapes=[
            pltpu.VMEM((128, 16, 128), f32),
            pltpu.VMEM((64, 128), f32),
            pltpu.VMEM((64, 128), f32),
        ],
        compiler_params=LIMIT,
        name="select",
    )(columns, kept.reshape(64, 128), kept)
    entries = lax.all_to_all(entries.reshape(128, 1, 128), ROWS, 0, 0, tiled=True)
    sketch = pl.pallas_call(
        turn_kernel,
        out_shape=jax.ShapeDtypeStruct((64, 256), f32),
        in_specs=[VMEM],
        out_specs=VMEM,
        name="turn",
    )(entries.reshape(128, 128))
    other = swap_cores(sketch)
    partial = pl.pallas_call(
        functools.partial(gram_kernel, 1.0 / 8192),
        out_shape=jax.ShapeDtypeStruct((640, 128), f32),
        in_specs=[SMEM, VMEM, VMEM],
        out_specs=VMEM,
        compiler_params=LIMIT,
        name="gram",
    )(column.reshape(1), sketch, other)
    share = jnp.sum(lax.all_to_all(partial.reshape(16, 40, 128), PLANE, 0, 0, tiled=True), axis=0)
    share = jnp.sum(copies(share, "rows_0", 8), axis=0)
    mine = copies(share, PLANE, 16).reshape(640, 128)
    theirs = swap_cores(mine)
    first = jnp.where(column == 0, mine, theirs)
    second = jnp.where(column == 0, theirs, mine)
    factor = jnp.linalg.cholesky(whole_gram(first, second)).T
    return sketch, lax.dynamic_slice_in_dim(factor, column * 256, 256, 1)


def solution(mesh):
    torus = Mesh(
        mesh.devices.reshape(8, 4, 4, mesh.shape["cols"]), ("rows_0", "rows_1", "rows_2", "cols")
    )
    return jax.shard_map(
        body,
        mesh=torus,
        in_specs=(P(ROWS, "cols"), P(ROWS), P()),
        out_specs=(P(ROWS, "cols"), P(None, "cols")),
        check_vma=False,
    )
```

time: 541 us -> 204 us (0.38)
  waiting for transfers between devices: 366 us -> 2.21 us
  blocking collectives: 6.39 us -> 96.7 us
  local copies, waits for them, and re-layouts: 39.6 us -> 5.26 us
  other arithmetic: 101 us -> 79.7 us
  between operations: 16.6 us -> 3.45 us
  Pallas kernels: 0 us -> 6.92 us
  starting transfers between devices: 0.16 us -> 6.99 us
    psum x1 -> x0, waiting for transfers between devices: 216 us -> none  [body(): gram = lax.psum(partial_gram, ROWS) / kept_total]
    reduce_scatter x3 -> x0, waiting for transfers between devices: 150 us -> none  [sum_by_axis(): so_far = lax.psum_scatter(so_far, axis, scatter_dimension=0, tiled=True)]
    all_to_all x1 -> x5, blocking collectives: 6.39 us -> 96.7 us  [the longest x1 44.7 us: body(): lax.all_to_all(local.reshape(128, 16, 128), ROWS, 0, 0, tiled=True)]
    gather x1 -> x0, local copies, waits for them, and re-layouts: 31.4 us -> none  [signed_rows(): return jnp.take(transformed, offsets, axis=0) * factor[:, None]]
    mul x8 -> x0, other arithmetic: 17.1 us -> none  [the longest x1 9.89 us: signed_rows(): return jnp.take(transformed, offsets, axis=0) * factor[:, None]]
    ppermute x0 -> x2, starting transfers between devices: none -> 6.99 us  [swap_cores(): return lax.ppermute(value, 'cols', [(0, 1), (1, 0)])]
    pallas_call x0 -> x4, Pallas kernels: none -> 6.92 us  [the longest x1 3.96 us: body(): pl.pallas_call(functools.partial(select_kernel, 1.0 / math.sqrt(131072)),...]
    another operation x14 -> x15, other arithmetic: 78.6 us -> 79.2 us  [body(): factor = jnp.linalg.cholesky(whole_gram(first, second)).T]
  transfers between devices with their start and end apart: 4 -> 2, of which waited for: 4 -> 2; matrix products, arithmetic and copies ran while one was open for 0% -> 0% of each run, Pallas kernels for 0% -> 0%
where the time goes in v1:
time: 204 us; the launch traced here: 203 us
  blocking collectives  96.7 us (47%)
  other arithmetic  79.7 us (39%)
  starting transfers between devices  6.99 us (3%)
  Pallas kernels  6.92 us (3%)
  local copies, waits for them, and re-layouts  5.26 us (3%)
  between operations  3.45 us (2%)
  waiting for transfers between devices  2.21 us (1%)
    another operation x15, other arithmetic, body(): factor = jnp.linalg.cholesky(whole_gram(first, second)).T  79.2 us
    all_to_all x1, blocking collectives, body(): lax.all_to_all(local.reshape(128, 16, 128), ROWS, 0, 0, tiled=True)  44.7 us
    all_to_all x2, blocking collectives, copies(): lax.all_to_all(jnp.broadcast_to(shard[None], (count, *shard.shape)), axes...  21.5 us
    all_to_all x1, blocking collectives, body(): lax.all_to_all(entries.reshape(128, 1, 128), ROWS, 0, 0, tiled=True)  18.9 us
    all_to_all x1, blocking collectives, body(): lax.all_to_all(partial.reshape(16, 40, 128), PLANE, 0, 0, tiled=True)  11.6 us
    ppermute x2, starting transfers between devices, swap_cores(): return lax.ppermute(value, 'cols', [(0, 1), (1, 0)])  6.99 us
  transfers between devices with their start and end apart: 2, of which 2 were waited for; matrix products, arithmetic and copies ran while one was open for 0% of the time, Pallas kernels for 0%

profile of v1, /device:TPU:1, one launch (start us, length us, event | category | flops | bytes accessed | tf_op | source)
XLA Modules:
  0.0 203.1 jit_solution(5560826347748091574)
XLA Ops:
  0.6 1.2 copy-done
  1.9 0.7 copy-done.3
  2.5 0.9 local_transform.1
  3.5 44.7 %all_to_all.25.columns_ref = f32[128,16,128]{2,1,0:T(8,128)S(1)} all-to-all(f32[128,16,128]{2,1,0:T(8,128)S(1)} %bitcast.45), channel_id=1, replica_groups=mesh['rows_0'=8,'rows_1'=4,'rows_2'=4,'cols'=2] {'rows_0','rows_1','rows..., dimensions={0} | all-to-all | bytes 2097152 | tf_op jit(solution)/shard_map/all_to_all | solution.py:176
  48.2 4.0 %select.29 = f32[128,128]{1,0:T(8,128)S(1)} custom-call(f32[128,16,128]{2,1,0:T(8,128)S(1)} %all_to_all.25.columns_ref, s32[64,128]{1,0:T(8,128)S(1)} %bitcast.48, s32[8192]{0:T(1024)S(1)} %copy-done.2), custom_call_target="tpu_custom_call" | custom-call | tf_op jit(solution)/shard_map/select/pallas_call | solution.py:177
  52.2 18.9 %all_to_all.26 = f32[128,1,128]{2,1,0:T(1,128)} all-to-all(f32[128,1,128]{2,1,0:T(1,128)S(1)} %bitcast.47), channel_id=1, replica_groups=mesh['rows_0'=8,'rows_1'=4,'rows_2'=4,'cols'=2] {'rows_0','rows_1','rows..., dimensions={0} | all-to-all | bytes 131072 | tf_op jit(solution)/shard_map/all_to_all | solution.py:190
  71.1 1.6 turn.1.own_ref
  72.7 3.1 %collective-permute-start = (f32[64,256]{1,0:T(8,128)}, f32[64,256]{1,0:T(8,128)S(1)}, u32[]{:S(2)}, u32[]{:S(2)}) collective-permute-start(f32[64,256]{1,0:T(8,128)} %turn.1.own_ref), channel_id=1, source_target_pairs={{0,1},{1,0},{2,3},{3,2},{4,5},{5,4},{6,7},{7,6},{8,9},{9,8},{10,11... | collective-permute-start | bytes 196616 | tf_op jit(solution)/shard_map/ppermute | solution.py:150
  75.8 1.1 collective-permute-done.other_ref
  76.9 0.8 copy-done.1
  78.2 11.6 %all_to_all.27 = f32[16,40,128]{2,1,0:T(8,128)S(1)} all-to-all(f32[16,40,128]{2,1,0:T(8,128)S(1)} %bitcast.46), channel_id=1, replica_groups=mesh['rows_0'=8,'rows_1'=4,'rows_2'=4,'cols'=2] {'rows_1','rows_2'}, dimensions={0} | all-to-all | bytes 655360 | tf_op jit(solution)/shard_map/all_to_all | solution.py:207
  89.8 10.4 %all_to_all.28 = f32[8,40,128]{2,1,0:T(8,128)S(1)} all-to-all(f32[8,40,128]{2,1,0:T(8,128)S(1)} %broadcast_in_dim.5), channel_id=1, replica_groups=mesh['rows_0'=8,'rows_1'=4,'rows_2'=4,'cols'=2] {'rows_0'}, dimensions={0} | all-to-all | bytes 327680 | tf_op jit(solution)/shard_map/all_to_all | solution.py:146
  100.3 11.0 %all_to_all.29 = f32[16,40,128]{2,1,0:T(8,128)S(1)} all-to-all(f32[16,40,128]{2,1,0:T(8,128)S(1)} %broadcast_in_dim.6), channel_id=1, replica_groups=mesh['rows_0'=8,'rows_1'=4,'rows_2'=4,'cols'=2] {'rows_1','rows_2'}, dimensions={0} | all-to-all | bytes 655360 | tf_op jit(solution)/shard_map/all_to_all | solution.py:146
  111.4 3.9 %collective-permute-start.1 = (f32[640,128]{1,0:T(8,128)S(1)}, f32[640,128]{1,0:T(8,128)S(1)}, u32[]{:S(2)}, u32[]{:S(2)}) collective-permute-start(f32[640,128]{1,0:T(8,128)S(1)} %bitcast.50), channel_id=1, source_target_pairs={{0,1},{1,0},{2,3},{3,2},{4,5},{5,4},{6,7},{7,6},{8,9},{9,8},{10,11... | collective-permute-start | bytes 983048 | tf_op jit(solution)/shard_map/ppermute | solution.py:150
  115.4 1.1 collective-permute-done.1
  118.1 11.7 %cholesky.104 = f32[128,128]{1,0:T(8,128)S(1)} custom-call(f32[128,128]{1,0:T(8,128)S(1)} %cholesky.266), custom_call_target="Cholesky" | custom-call | tf_op jit(solution)/shard_map/jit(cholesky)/cholesky | solution.py:213
  130.7 9.8 %custom-call.27 = f32[1,128,128]{1,2,0:T(8,128)S(1)} custom-call(f32[1,128,128]{2,1,0:T(8,128)S(1)} %get-tuple-element.31), custom_call_target="InvertDiagBlocksLowerTriangular" | custom-call | tf_op jit(solution)/shard_map/jit(cholesky)/cholesky | solution.py:213
  141.1 11.7 %cholesky.217 = f32[128,128]{1,0:T(8,128)S(1)} custom-call(f32[128,128]{1,0:T(8,128)S(1)} %cholesky.270), custom_call_target="Cholesky" | custom-call | tf_op jit(solution)/shard_map/jit(cholesky)/cholesky | solution.py:213
  152.9 0.7 compare_reduce_fusion.2
  153.6 10.0 %custom-call.28 = f32[1,128,128]{1,2,0:T(8,128)S(1)} custom-call(f32[1,128,128]{2,1,0:T(8,128)S(1)} %get-tuple-element.28), custom_call_target="InvertDiagBlocksLowerTriangular" | custom-call | tf_op jit(solution)/shard_map/jit(cholesky)/cholesky | solution.py:213
  164.2 11.7 %cholesky.238 = f32[128,128]{1,0:T(8,128)S(1)} custom-call(f32[128,128]{1,0:T(8,128)S(1)} %cholesky.275), custom_call_target="Cholesky" | custom-call | tf_op jit(solution)/shard_map/jit(cholesky)/cholesky | solution.py:213
  176.6 9.8 %custom-call.29 = f32[1,128,128]{1,2,0:T(8,128)S(1)} custom-call(f32[1,128,128]{2,1,0:T(8,128)S(1)} %get-tuple-element.25), custom_call_target="InvertDiagBlocksLowerTriangular" | custom-call | tf_op jit(solution)/shard_map/jit(cholesky)/cholesky | solution.py:213
  187.0 11.7 %cholesky.255 = f32[128,128]{1,0:T(8,128)S(1)} custom-call(f32[128,128]{1,0:T(8,128)S(1)} %convolution_subtract_fusion.2), custom_call_target="Cholesky" | custom-call | tf_op jit(solution)/shard_map/jit(cholesky)/cholesky | solution.py:213
  202.1 1.0 copy.39
  (44 shorter events, 6.4 us)
Async XLA Ops:
  0.6 1.2 copy-start
  1.9 0.7 copy-start.3
  3.5 44.7 %copy-start.2 = (s32[8192]{0:T(1024)S(1)}, s32[8192]{0:T(1024)}, u32[]{:S(2)}) copy-start(s32[8192]{0:T(1024)} %kept_scalar_ref.1) | copy-start | bytes 98308
  72.7 4.2 %collective-permute-start = (f32[64,256]{1,0:T(8,128)}, f32[64,256]{1,0:T(8,128)S(1)}, u32[]{:S(2)}, u32[]{:S(2)}) collective-permute-start(f32[64,256]{1,0:T(8,128)} %turn.1.own_ref), channel_id=1, source_target_pairs={{0,1},{1,0},{2,3},{3,2},{4,5},{5,4},{6,7},{7,6},{8,9},{9,8},{10,11... | collective-permute-start | bytes 196616 | tf_op jit(solution)/shard_map/ppermute | solution.py:150
  76.9 0.8 copy-start.1
  111.4 5.2 %collective-permute-start.1 = (f32[640,128]{1,0:T(8,128)S(1)}, f32[640,128]{1,0:T(8,128)S(1)}, u32[]{:S(2)}, u32[]{:S(2)}) collective-permute-start(f32[640,128]{1,0:T(8,128)S(1)} %bitcast.50), channel_id=1, source_target_pairs={{0,1},{1,0},{2,3},{3,2},{4,5},{5,4},{6,7},{7,6},{8,9},{9,8},{10,11... | collective-permute-start | bytes 983048 | tf_op jit(solution)/shard_map/ppermute | solution.py:150

commit v2 on v1

--- a/solution.py
+++ b/solution.py
@@ -150,16 +150,79 @@
     return lax.ppermute(value, "cols", [(0, 1), (1, 0)])
 
 
-def whole_gram(first, second):
-    b = [first[i * 128 : (i + 1) * 128] for i in range(5)]
-    d = [second[i * 128 : (i + 1) * 128] for i in range(5)]
-    rows = [
-        [b[0], b[1], b[3], b[4]],
-        [b[1].T, b[2], d[3], d[4]],
-        [b[3].T, d[3].T, d[0], d[1]],
-        [b[4].T, d[4].T, d[1].T, d[2]],
-    ]
-    return jnp.concatenate([jnp.concatenate(r, 1) for r in rows], 0)
+def high_dot(a, b, dims):
+    return lax.dot_general(a, b, (dims, ((), ())), precision=lax.Precision.HIGHEST, preferred_element_type=jnp.float32)
+
+
+def spread(row):
+    return jnp.broadcast_to(row, (8, 128))
+
+
+def factor_block(block, upper_ref, inverse_ref):
+    lanes = lax.broadcasted_iota(jnp.int32, (8, 128), 1)
+    strips = [block[8 * s : 8 * s + 8] for s in range(16)]
+    for s in range(16):
+        here = strips[s]
+        base = 8 * s
+        inside = (lanes >= base) & (lanes < base + 8)
+        columns = [spread(here[:, base + k : base + k + 1]) for k in range(8)]
+        e = [[spread(columns[k][i : i + 1]) if k >= i else None for k in range(8)] for i in range(8)]
+        m = [jnp.where(inside, jnp.where(lanes == base + k, 1.0, 0.0), spread(here[k : k + 1])) for k in range(8)]
+        d, u, r = [None] * 8, [[None] * 8 for _ in range(8)], [None] * 8
+        for k in range(8):
+            d[k] = lax.rsqrt(e[k][k])
+            for j in range(k + 1, 8):
+                u[k][j] = e[k][j] * d[k]
+            r[k] = m[k] * d[k]
+            for i in range(k + 1, 8):
+                for j in range(i, 8):
+                    e[i][j] = e[i][j] - u[k][i] * u[k][j]
+            for i in range(k + 1, 8):
+                m[i] = m[i] - u[k][i] * r[k]
+        z = [None] * 8
+        for k in reversed(range(8)):
+            z[k] = r[k] * d[k]
+            for j in reversed(range(k + 1, 8)):
+                z[k] = z[k] - (u[k][j] * d[k]) * z[j]
+        for t in range(s + 1, 16):
+            there = strips[t]
+            total = jnp.where(inside, 0.0, there)
+            for k in range(8):
+                total = total - spread(there[:, base + k : base + k + 1]) * z[k]
+            strips[t] = total
+        for k in range(8):
+            row = r[k]
+            inverse_ref[base + k : base + k + 1, :] = jnp.where(lanes < base + 8, row, 0.0)[:1]
+            row = jnp.where(lanes < base + 8, 0.0, row)
+            row = jnp.where(lanes == base + k, e[k][k] * d[k], row)
+            for j in range(k + 1, 8):
+                row = jnp.where(lanes == base + j, u[k][j], row)
+            upper_ref[base + k : base + k + 1, :] = row[:1]
+
+
+def cholesky_kernel(column_ref, mine_ref, theirs_ref, out_ref, gram, upper, inverse):
+    zero = column_ref[0] == 0
+    names = [(0, 0), (0, 1), (1, 1), (0, 2), (0, 3), (2, 2), (2, 3), (3, 3), (1, 2), (1, 3)]
+    place = {name: i for i, name in enumerate(names)}
+    a = {}
+    for i in range(5):
+        x, y = mine_ref[i * 128 : i * 128 + 128, :], theirs_ref[i * 128 : i * 128 + 128, :]
+        a[names[i]] = jnp.where(zero, x, y)
+        a[names[5 + i]] = jnp.where(zero, y, x)
+    for name in names:
+        gram[place[name]] = a[name]
+    for p in range(4):
+        factor_block(gram[place[p, p]], upper.at[p * 4 + p], inverse)
+        for q in range(p + 1, 4):
+            upper[p * 4 + q] = high_dot(inverse[...], gram[place[p, q]], ((1,), (0,)))
+        for i in range(p + 1, 4):
+            for j in range(i, 4):
+                gram[place[i, j]] = gram[place[i, j]] - high_dot(upper[p * 4 + i], upper[p * 4 + j], ((0,), (0,)))
+        for q in range(p):
+            upper[p * 4 + q] = jnp.zeros((128, 128), jnp.float32)
+    for p in range(4):
+        for h in range(2):
+            out_ref[p * 128 : p * 128 + 128, h * 128 : h * 128 + 128] = jnp.where(zero, upper[p * 4 + h], upper[p * 4 + 2 + h])
 
 
 def body(design, signs, kept):
@@ -208,10 +271,20 @@
     share = jnp.sum(copies(share, "rows_0", 8), axis=0)
     mine = copies(share, PLANE, 16).reshape(640, 128)
     theirs = swap_cores(mine)
-    first = jnp.where(column == 0, mine, theirs)
-    second = jnp.where(column == 0, theirs, mine)
-    factor = jnp.linalg.cholesky(whole_gram(first, second)).T
-    return sketch, lax.dynamic_slice_in_dim(factor, column * 256, 256, 1)
+    factor = pl.pallas_call(
+        cholesky_kernel,
+        out_shape=jax.ShapeDtypeStruct((512, 256), f32),
+        in_specs=[SMEM, VMEM, VMEM],
+        out_specs=VMEM,
+        scratch_shapes=[
+            pltpu.VMEM((10, 128, 128), f32),
+            pltpu.VMEM((16, 128, 128), f32),
+            pltpu.VMEM((128, 128), f32),
+        ],
+        compiler_params=LIMIT,
+        name="cholesky",
+    )(column.reshape(1), mine, theirs)
+    return sketch, factor
 
 
 def solution(mesh):

time: 204 us -> 139 us (0.68)
  other arithmetic: 79.7 us -> 0.04 us
  Pallas kernels: 6.92 us -> 29.6 us
  between operations: 3.45 us -> 0.7 us
  local copies, waits for them, and re-layouts: 5.26 us -> 2.79 us
    another operation x15 -> x0, other arithmetic: 79.2 us -> none  [body(): factor = jnp.linalg.cholesky(whole_gram(first, second)).T]
    pallas_call x0 -> x1, Pallas kernels: none -> 22.7 us  [body(): pl.pallas_call(cholesky_kernel, out_shape=jax.ShapeDtypeStruct((512, 256)...]
where the time goes in v2:
time: 139 us
  blocking collectives  96.9 us (70%)
  Pallas kernels  29.6 us (21%)
  starting transfers between devices  6.6 us (5%)
  local copies, waits for them, and re-layouts  2.79 us (2%)
  waiting for transfers between devices  2.37 us (2%)
    all_to_all x1, blocking collectives, body(): lax.all_to_all(local.reshape(128, 16, 128), ROWS, 0, 0, tiled=True)  44.7 us
    pallas_call x1, Pallas kernels, body(): pl.pallas_call(cholesky_kernel, out_shape=jax.ShapeDtypeStruct((512, 256)...  22.7 us
    all_to_all x2, blocking collectives, copies(): lax.all_to_all(jnp.broadcast_to(shard[None], (count, *shard.shape)), axes...  21.5 us
    all_to_all x1, blocking collectives, body(): lax.all_to_all(entries.reshape(128, 1, 128), ROWS, 0, 0, tiled=True)  19.1 us
    all_to_all x1, blocking collectives, body(): lax.all_to_all(partial.reshape(16, 40, 128), PLANE, 0, 0, tiled=True)  11.6 us
    ppermute x2, starting transfers between devices, swap_cores(): return lax.ppermute(value, 'cols', [(0, 1), (1, 0)])  6.6 us
    pallas_call x1, Pallas kernels, body(): pl.pallas_call(functools.partial(select_kernel, 1.0 / math.sqrt(131072)),...  3.96 us
  transfers between devices with their start and end apart: 2, of which 2 were waited for; matrix products, arithmetic and copies ran while one was open for 0% of the time, Pallas kernels for 0%

profile of v2, /device:TPU:1, one launch (start us, length us, event | category | flops | bytes accessed | tf_op | source)
XLA Modules:
  0.0 139.0 jit_solution(4404009573335951338)
XLA Ops:
  0.6 0.0 copy-start
  0.6 1.2 copy-done
  1.9 0.0 copy-start.3
  1.9 0.7 copy-done.3
  2.5 0.9 local_transform.1
  3.5 0.0 copy-start.2
  3.5 44.7 %all_to_all.25.columns_ref = f32[128,16,128]{2,1,0:T(8,128)S(1)} all-to-all(f32[128,16,128]{2,1,0:T(8,128)S(1)} %bitcast.10), channel_id=1, replica_groups=mesh['rows_0'=8,'rows_1'=4,'rows_2'=4,'cols'=2] {'rows_0','rows_1','rows..., dimensions={0} | all-to-all | bytes 2097152 | tf_op jit(solution)/shard_map/all_to_all | solution.py:239
  48.2 0.0 copy-done.2
  48.2 4.0 %select.1 = f32[128,128]{1,0:T(8,128)S(1)} custom-call(f32[128,16,128]{2,1,0:T(8,128)S(1)} %all_to_all.25.columns_ref, s32[64,128]{1,0:T(8,128)S(1)} %bitcast.15, s32[8192]{0:T(1024)S(1)} %copy-done.2), custom_call_target="tpu_custom_call" | custom-call | tf_op jit(solution)/shard_map/select/pallas_call | solution.py:240
  52.2 19.1 %all_to_all.26 = f32[128,1,128]{2,1,0:T(1,128)} all-to-all(f32[128,1,128]{2,1,0:T(1,128)S(1)} %bitcast.14), channel_id=1, replica_groups=mesh['rows_0'=8,'rows_1'=4,'rows_2'=4,'cols'=2] {'rows_0','rows_1','rows..., dimensions={0} | all-to-all | bytes 131072 | tf_op jit(solution)/shard_map/all_to_all | solution.py:253
  71.3 1.6 %turn.1.own_ref = f32[64,256]{1,0:T(8,128)} custom-call(f32[128,128]{1,0:T(8,128)} %bitcast.17), custom_call_target="tpu_custom_call" | custom-call | tf_op jit(solution)/shard_map/turn/pallas_call | solution.py:254
  72.8 2.7 %collective-permute-start = (f32[64,256]{1,0:T(8,128)}, f32[64,256]{1,0:T(8,128)S(1)}, u32[]{:S(2)}, u32[]{:S(2)}) collective-permute-start(f32[64,256]{1,0:T(8,128)} %turn.1.own_ref), channel_id=1, source_target_pairs={{0,1},{1,0},{2,3},{3,2},{4,5},{5,4},{6,7},{7,6},{8,9},{9,8},{10,11... | collective-permute-start | bytes 196616 | tf_op jit(solution)/shard_map/ppermute | solution.py:150
  75.5 1.1 collective-permute-done.other_ref
  76.6 0.0 copy-start.1
  76.7 0.8 copy-done.1
  77.5 0.5 gram.1
  78.0 11.6 %all_to_all.27 = f32[16,40,128]{2,1,0:T(8,128)S(1)} all-to-all(f32[16,40,128]{2,1,0:T(8,128)S(1)} %bitcast.11), channel_id=1, replica_groups=mesh['rows_0'=8,'rows_1'=4,'rows_2'=4,'cols'=2] {'rows_1','rows_2'}, dimensions={0} | all-to-all | bytes 655360 | tf_op jit(solution)/shard_map/all_to_all | solution.py:270
  89.6 10.4 %all_to_all.28 = f32[8,40,128]{2,1,0:T(8,128)S(1)} all-to-all(f32[8,40,128]{2,1,0:T(8,128)S(1)} %broadcast_in_dim.4), channel_id=1, replica_groups=mesh['rows_0'=8,'rows_1'=4,'rows_2'=4,'cols'=2] {'rows_0'}, dimensions={0} | all-to-all | bytes 327680 | tf_op jit(solution)/shard_map/all_to_all | solution.py:146
  100.1 11.0 %all_to_all.29 = f32[16,40,128]{2,1,0:T(8,128)S(1)} all-to-all(f32[16,40,128]{2,1,0:T(8,128)S(1)} %broadcast_in_dim.5), channel_id=1, replica_groups=mesh['rows_0'=8,'rows_1'=4,'rows_2'=4,'cols'=2] {'rows_1','rows_2'}, dimensions={0} | all-to-all | bytes 655360 | tf_op jit(solution)/shard_map/all_to_all | solution.py:146
  111.1 3.9 %collective-permute-start.1 = (f32[640,128]{1,0:T(8,128)S(1)}, f32[640,128]{1,0:T(8,128)S(1)}, u32[]{:S(2)}, u32[]{:S(2)}) collective-permute-start(f32[640,128]{1,0:T(8,128)S(1)} %bitcast.12), channel_id=1, source_target_pairs={{0,1},{1,0},{2,3},{3,2},{4,5},{5,4},{6,7},{7,6},{8,9},{9,8},{10,11... | collective-permute-start | bytes 983048 | tf_op jit(solution)/shard_map/ppermute | solution.py:150
  115.0 1.3 collective-permute-done.1.theirs_ref
  116.3 22.7 %cholesky.1 = f32[512,256]{1,0:T(8,128)} custom-call(s32[1]{0:T(128)} %bitcast.6.column_ref, f32[640,128]{1,0:T(8,128)S(1)} %bitcast.13, f32[640,128]{1,0:T(8,128)S(1)} %collective-permute-done.1.theirs_ref), custom_call_target="tpu_custom_call" | custom-call | tf_op jit(solution)/shard_map/cholesky/pallas_call | solution.py:274
  (4 shorter events, 0.1 us)
Async XLA Ops:
  0.6 1.2 copy-start
  1.9 0.7 copy-start.3
  3.5 44.7 %copy-start.2 = (s32[8192]{0:T(1024)S(1)}, s32[8192]{0:T(1024)}, u32[]{:S(2)}) copy-start(s32[8192]{0:T(1024)} %kept_scalar_ref.1) | copy-start | bytes 98308
  72.8 3.8 %collective-permute-start = (f32[64,256]{1,0:T(8,128)}, f32[64,256]{1,0:T(8,128)S(1)}, u32[]{:S(2)}, u32[]{:S(2)}) collective-permute-start(f32[64,256]{1,0:T(8,128)} %turn.1.own_ref), channel_id=1, source_target_pairs={{0,1},{1,0},{2,3},{3,2},{4,5},{5,4},{6,7},{7,6},{8,9},{9,8},{10,11... | collective-permute-start | bytes 196616 | tf_op jit(solution)/shard_map/ppermute | solution.py:150
  76.6 0.8 copy-start.1
  111.1 5.2 %collective-permute-start.1 = (f32[640,128]{1,0:T(8,128)S(1)}, f32[640,128]{1,0:T(8,128)S(1)}, u32[]{:S(2)}, u32[]{:S(2)}) collective-permute-start(f32[640,128]{1,0:T(8,128)S(1)} %bitcast.12), channel_id=1, source_target_pairs={{0,1},{1,0},{2,3},{3,2},{4,5},{5,4},{6,7},{7,6},{8,9},{9,8},{10,11... | collective-permute-start | bytes 983048 | tf_op jit(solution)/shard_map/ppermute | solution.py:150

commit v3 on v2

--- a/solution.py
+++ b/solution.py
@@ -15,6 +15,8 @@
 SMEM = pl.BlockSpec(memory_space=pltpu.SMEM)
 LIMIT = pltpu.CompilerParams(vmem_limit_bytes=32 * 1024 * 1024)
 WINDOW = 4
+GROUP = 1
+AHEAD = 2
 
 
 def butterflies(values):
@@ -37,22 +39,27 @@
     return (1 - 2 * (parity & 1)).astype(jnp.float32).astype(jnp.bfloat16)
 
 
-def local_kernel(design_ref, signs_ref, out_ref):
+def local_kernel(design_ref, signs_ref, out_ref, held, sems):
+    def fetch(b):
+        rows = pl.ds(b * 128, 128)
+        return pltpu.make_async_copy(design_ref.at[rows, :], held.at[rows, :], sems.at[b])
+
+    for b in range(8):
+        fetch(b).start()
     table = sylvester(128)
-    for half in range(2):
-        parts = []
-        for b in range(8):
-            piece = design_ref[b * 128 : (b + 1) * 128, half * 128 : (half + 1) * 128].T
-            piece = piece * signs_ref[b : b + 1, :].astype(jnp.float32)
-            high = piece.astype(jnp.bfloat16)
-            rest = piece - high.astype(jnp.float32)
-            middle = rest.astype(jnp.bfloat16)
-            low = (rest - middle.astype(jnp.float32)).astype(jnp.bfloat16)
+    parts = [[], []]
+    for b in range(8):
+        fetch(b).wait()
+        sign = signs_ref[b : b + 1, :].astype(jnp.float32)
+        for half in range(2):
+            piece = held[b * 128 : (b + 1) * 128, half * 128 : (half + 1) * 128].T * sign
+            high, middle, low = thirds(piece)
             total = jnp.dot(low, table, preferred_element_type=jnp.float32)
             total += jnp.dot(middle, table, preferred_element_type=jnp.float32)
             total += jnp.dot(high, table, preferred_element_type=jnp.float32)
-            parts.append(total)
-        for q, mixed in enumerate(butterflies(parts)):
+            parts[half].append(total)
+    for half in range(2):
+        for q, mixed in enumerate(butterflies(parts[half])):
             out_ref[pl.ds(half * 8 + q, 128, stride=16), :] = mixed
 
 
@@ -114,15 +121,12 @@
     out_ref[pl.ds(1, 64, stride=2), :] = jnp.where(left, pltpu.roll(a, 64, 1), b)
 
 
-def turn_kernel(entries_ref, sketch_ref):
-    turned = entries_ref[...].T
-    sketch_ref[:, :128] = turned[:64]
-    sketch_ref[:, 128:] = turned[64:]
-
-
-def gram_kernel(scale, column_ref, own_ref, other_ref, out_ref):
-    own = [own_ref[:, :128], own_ref[:, 128:]]
-    other = [other_ref[:, :128], other_ref[:, 128:]]
+def gram_kernel(scale, column_ref, mine_ref, theirs_ref, sketch_ref, out_ref):
+    turned, theirs = mine_ref[...].T, theirs_ref[...].T
+    own = [turned[:64], turned[64:]]
+    other = [theirs[:64], theirs[64:]]
+    sketch_ref[:, :128] = own[0]
+    sketch_ref[:, 128:] = own[1]
     zero = column_ref[0] == 0
 
     def choose(a, b):
@@ -150,24 +154,53 @@
     return lax.ppermute(value, "cols", [(0, 1), (1, 0)])
 
 
-def high_dot(a, b, dims):
-    return lax.dot_general(a, b, (dims, ((), ())), precision=lax.Precision.HIGHEST, preferred_element_type=jnp.float32)
+def thirds(value):
+    high = value.astype(jnp.bfloat16)
+    rest = value - high.astype(jnp.float32)
+    middle = rest.astype(jnp.bfloat16)
+    return high, middle, (rest - middle.astype(jnp.float32)).astype(jnp.bfloat16)
+
+
+def product(left, right):
+    (ah, am, al), (bh, bm, bl) = left, right
+    top = jnp.concatenate([bh, bm], 0)
+
+    def dot(a, b):
+        return lax.dot_general(a, b, (((1,), (0,)), ((), ())), preferred_element_type=jnp.float32)
+
+    small = dot(jnp.concatenate([ah, al], 1), jnp.concatenate([bl, bh], 0))
+    small = small + dot(jnp.concatenate([am, am], 1), top)
+    return small + dot(jnp.concatenate([ah, ah], 1), top)
 
 
 def spread(row):
     return jnp.broadcast_to(row, (8, 128))
 
 
-def factor_block(block, upper_ref, inverse_ref):
+def block_product(left, right):
+    ah, am, al = thirds(left)
+    bh, bm, bl = thirds(right)
+    return lax.dot_general(
+        jnp.concatenate([ah, am, ah, am, al, ah], 0),
+        jnp.concatenate([bh, bh, bm, bm, bh, bl], 0),
+        (((0,), (0,)), ((), ())),
+        preferred_element_type=jnp.float32,
+    )
+
+
+def factor_block(block, upper_ref, inverse_ref, rows_ref, entries_ref, later):
     lanes = lax.broadcasted_iota(jnp.int32, (8, 128), 1)
     strips = [block[8 * s : 8 * s + 8] for s in range(16)]
     for s in range(16):
         here = strips[s]
         base = 8 * s
+        rows, entries = rows_ref.at[s % 2], entries_ref.at[s % 2]
         inside = (lanes >= base) & (lanes < base + 8)
-        columns = [spread(here[:, base + k : base + k + 1]) for k in range(8)]
-        e = [[spread(columns[k][i : i + 1]) if k >= i else None for k in range(8)] for i in range(8)]
-        m = [jnp.where(inside, jnp.where(lanes == base + k, 1.0, 0.0), spread(here[k : k + 1])) for k in range(8)]
+        rows[...] = here
+        for k in range(8):
+            entries[8 * k : 8 * k + 8] = spread(here[:, base + k : base + k + 1])
+        e = [[entries[pl.ds(8 * k + i, 8, stride=0), :] if k >= i else None for k in range(8)] for i in range(8)]
+        m = [jnp.where(inside, jnp.where(lanes == base + k, 1.0, 0.0), rows[pl.ds(k, 8, stride=0), :]) for k in range(8)]
         d, u, r = [None] * 8, [[None] * 8 for _ in range(8)], [None] * 8
         for k in range(8):
             d[k] = lax.rsqrt(e[k][k])
@@ -184,7 +217,8 @@
             z[k] = r[k] * d[k]
             for j in reversed(range(k + 1, 8)):
                 z[k] = z[k] - (u[k][j] * d[k]) * z[j]
-        for t in range(s + 1, 16):
+        end = (s // GROUP + 1) * GROUP
+        for t in range(s + 1, min(end + AHEAD, 16)):
             there = strips[t]
             total = jnp.where(inside, 0.0, there)
             for k in range(8):
@@ -198,28 +232,48 @@
             for j in range(k + 1, 8):
                 row = jnp.where(lanes == base + j, u[k][j], row)
             upper_ref[base + k : base + k + 1, :] = row[:1]
-
-
-def cholesky_kernel(column_ref, mine_ref, theirs_ref, out_ref, gram, upper, inverse):
+        if later:
+            later.pop(0)()
+        if s + 1 == end and end + AHEAD < 16:
+            first, last = 8 * (end - GROUP), 8 * end
+            group = lanes[:1] < last
+            u_rows = upper_ref[first:last, :]
+            delta = block_product(u_rows, jnp.where(group, inverse_ref[first:last, :], u_rows))
+            group = (lanes >= first) & (lanes < last)
+            for t in range(end + AHEAD, 16):
+                strips[t] = jnp.where(group, 0.0, strips[t]) - delta[8 * t : 8 * t + 8]
+
+
+def cholesky_kernel(column_ref, mine_ref, theirs_ref, out_ref, gram, upper, inverse, rows_ref, entries_ref):
     zero = column_ref[0] == 0
     names = [(0, 0), (0, 1), (1, 1), (0, 2), (0, 3), (2, 2), (2, 3), (3, 3), (1, 2), (1, 3)]
     place = {name: i for i, name in enumerate(names)}
-    a = {}
     for i in range(5):
         x, y = mine_ref[i * 128 : i * 128 + 128, :], theirs_ref[i * 128 : i * 128 + 128, :]
-        a[names[i]] = jnp.where(zero, x, y)
-        a[names[5 + i]] = jnp.where(zero, y, x)
-    for name in names:
-        gram[place[name]] = a[name]
+        gram[i] = jnp.where(zero, x, y)
+        gram[5 + i] = jnp.where(zero, y, x)
+
+    def solve(p, q):
+        upper[p * 4 + q] = product(thirds(inverse[p]), thirds(gram[place[p, q]]))
+
+    def update(p, i, j):
+        gram[place[i, j]] -= product(thirds(upper[p * 4 + i].T), thirds(upper[p * 4 + j]))
+
+    later = []
     for p in range(4):
-        factor_block(gram[place[p, p]], upper.at[p * 4 + p], inverse)
-        for q in range(p + 1, 4):
-            upper[p * 4 + q] = high_dot(inverse[...], gram[place[p, q]], ((1,), (0,)))
-        for i in range(p + 1, 4):
-            for j in range(i, 4):
-                gram[place[i, j]] = gram[place[i, j]] - high_dot(upper[p * 4 + i], upper[p * 4 + j], ((0,), (0,)))
+        factor_block(gram[place[p, p]], upper.at[p * 4 + p], inverse.at[p], rows_ref, entries_ref, later)
+        for work in later:
+            work()
+        later = []
         for q in range(p):
             upper[p * 4 + q] = jnp.zeros((128, 128), jnp.float32)
+        if p < 3:
+            solve(p, p + 1)
+            update(p, p + 1, p + 1)
+        for j in range(p + 2, 4):
+            later.append(functools.partial(solve, p, j))
+            for i in range(p + 1, j + 1):
+                later.append(functools.partial(update, p, i, j))
     for p in range(4):
         for h in range(2):
             out_ref[p * 128 : p * 128 + 128, h * 128 : h * 128 + 128] = jnp.where(zero, upper[p * 4 + h], upper[p * 4 + 2 + h])
@@ -231,9 +285,10 @@
     local = pl.pallas_call(
         local_kernel,
         out_shape=jax.ShapeDtypeStruct((2048, 128), f32),
-        in_specs=[VMEM, VMEM],
+        in_specs=[pl.BlockSpec(memory_space=pltpu.HBM), VMEM],
         out_specs=VMEM,
-        compiler_params=LIMIT,
+        scratch_shapes=[pltpu.VMEM((1024, 256), f32), pltpu.SemaphoreType.DMA((8,))],
+        compiler_params=pltpu.CompilerParams(vmem_limit_bytes=60 * 1024 * 1024),
         name="local_transform",
     )(design, signs.reshape(8, 128))
     columns = lax.all_to_all(local.reshape(128, 16, 128), ROWS, 0, 0, tiled=True)
@@ -251,22 +306,15 @@
         name="select",
     )(columns, kept.reshape(64, 128), kept)
     entries = lax.all_to_all(entries.reshape(128, 1, 128), ROWS, 0, 0, tiled=True)
-    sketch = pl.pallas_call(
-        turn_kernel,
-        out_shape=jax.ShapeDtypeStruct((64, 256), f32),
-        in_specs=[VMEM],
-        out_specs=VMEM,
-        name="turn",
-    )(entries.reshape(128, 128))
-    other = swap_cores(sketch)
-    partial = pl.pallas_call(
+    entries = entries.reshape(128, 128)
+    sketch, partial = pl.pallas_call(
         functools.partial(gram_kernel, 1.0 / 8192),
-        out_shape=jax.ShapeDtypeStruct((640, 128), f32),
+        out_shape=(jax.ShapeDtypeStruct((64, 256), f32), jax.ShapeDtypeStruct((640, 128), f32)),
         in_specs=[SMEM, VMEM, VMEM],
-        out_specs=VMEM,
+        out_specs=(VMEM, VMEM),
         compiler_params=LIMIT,
         name="gram",
-    )(column.reshape(1), sketch, other)
+    )(column.reshape(1), entries, swap_cores(entries))
     share = jnp.sum(lax.all_to_all(partial.reshape(16, 40, 128), PLANE, 0, 0, tiled=True), axis=0)
     share = jnp.sum(copies(share, "rows_0", 8), axis=0)
     mine = copies(share, PLANE, 16).reshape(640, 128)
@@ -279,7 +327,9 @@
         scratch_shapes=[
             pltpu.VMEM((10, 128, 128), f32),
             pltpu.VMEM((16, 128, 128), f32),
-            pltpu.VMEM((128, 128), f32),
+            pltpu.VMEM((4, 128, 128), f32),
+            pltpu.VMEM((2, 8, 128), f32),
+            pltpu.VMEM((2, 64, 128), f32),
         ],
         compiler_params=LIMIT,
         name="cholesky",

time: 139 us -> 131 us (0.942)
  Pallas kernels: 29.6 us -> 24.7 us
  local copies, waits for them, and re-layouts: 2.79 us -> 0.04 us
    pallas_call x1, Pallas kernels: 22.7 us -> 14.9 us  [body(): pl.pallas_call(cholesky_kernel, out_shape=jax.ShapeDtypeStruct((512, 256)...]
    pallas_call x1, Pallas kernels: 0.94 us -> 5.15 us  [body(): pl.pallas_call(local_kernel, out_shape=jax.ShapeDtypeStruct((2048, 128),...]
    unnamed x8 -> x2, local copies, waits for them, and re-layouts: 2.75 us -> 0.01 us
where the time goes in v3:
time: 131 us
  blocking collectives  96.6 us (74%)
  Pallas kernels  24.7 us (19%)
  starting transfers between devices  6.68 us (5%)
  waiting for transfers between devices  2.16 us (2%)
    all_to_all x1, blocking collectives, body(): lax.all_to_all(local.reshape(128, 16, 128), ROWS, 0, 0, tiled=True)  45 us
    all_to_all x2, blocking collectives, copies(): lax.all_to_all(jnp.broadcast_to(shard[None], (count, *shard.shape)), axes...  21.4 us
    all_to_all x1, blocking collectives, body(): lax.all_to_all(entries.reshape(128, 1, 128), ROWS, 0, 0, tiled=True)  18.6 us
    pallas_call x1, Pallas kernels, body(): pl.pallas_call(cholesky_kernel, out_shape=jax.ShapeDtypeStruct((512, 256)...  14.9 us
    all_to_all x1, blocking collectives, body(): lax.all_to_all(partial.reshape(16, 40, 128), PLANE, 0, 0, tiled=True)  11.6 us
    ppermute x2, starting transfers between devices, swap_cores(): return lax.ppermute(value, 'cols', [(0, 1), (1, 0)])  6.68 us
    pallas_call x1, Pallas kernels, body(): pl.pallas_call(local_kernel, out_shape=jax.ShapeDtypeStruct((2048, 128),...  5.15 us
    pallas_call x1, Pallas kernels, body(): pl.pallas_call(functools.partial(select_kernel, 1.0 / math.sqrt(131072)),...  3.96 us
  transfers between devices with their start and end apart: 2, of which 2 were waited for; matrix products, arithmetic and copies ran while one was open for 0% of the time, Pallas kernels for 0%

profile of v3, /device:TPU:1, one launch (start us, length us, event | category | flops | bytes accessed | tf_op | source)
XLA Modules:
  0.0 130.9 jit_solution(8136218404799335941)
XLA Ops:
  0.6 5.1 %local_transform.1 = f32[2048,128]{1,0:T(8,128)} custom-call(f32[1024,256]{1,0:T(8,128)} %design_ref.1, s32[8,128]{1,0:T(8,128)} %bitcast.18), custom_call_target="tpu_custom_call" | custom-call | tf_op jit(solution)/shard_map/local_transform/pallas_call | solution.py:285
  5.8 0.0 copy-start
  5.8 45.0 %all_to_all.25.columns_ref = f32[128,16,128]{2,1,0:T(8,128)S(1)} all-to-all(f32[128,16,128]{2,1,0:T(8,128)} %bitcast.17), channel_id=1, replica_groups=mesh['rows_0'=8,'rows_1'=4,'rows_2'=4,'cols'=2] {'rows_0','rows_1','rows..., dimensions={0} | all-to-all | bytes 2097152 | tf_op jit(solution)/shard_map/all_to_all | solution.py:294
  50.8 0.0 copy-done
  50.8 4.0 %select.1 = f32[128,128]{1,0:T(8,128)S(1)} custom-call(f32[128,16,128]{2,1,0:T(8,128)S(1)} %all_to_all.25.columns_ref, s32[64,128]{1,0:T(8,128)S(1)} %bitcast.16, s32[8192]{0:T(1024)S(1)} %copy-done), custom_call_target="tpu_custom_call" | custom-call | tf_op jit(solution)/shard_map/select/pallas_call | solution.py:295
  54.7 18.6 %all_to_all.26 = f32[128,1,128]{2,1,0:T(1,128)S(1)} all-to-all(f32[128,1,128]{2,1,0:T(1,128)S(1)} %bitcast.13), channel_id=1, replica_groups=mesh['rows_0'=8,'rows_1'=4,'rows_2'=4,'cols'=2] {'rows_0','rows_1','rows..., dimensions={0} | all-to-all | bytes 131072 | tf_op jit(solution)/shard_map/all_to_all | solution.py:308
  73.3 2.8 %collective-permute-start = (f32[128,128]{1,0:T(8,128)S(1)}, f32[128,128]{1,0:T(8,128)S(1)}, u32[]{:S(2)}, u32[]{:S(2)}) collective-permute-start(f32[128,128]{1,0:T(8,128)S(1)} %bitcast.14), channel_id=1, source_target_pairs={{0,1},{1,0},{2,3},{3,2},{4,5},{5,4},{6,7},{7,6},{8,9},{9,8},{10,11... | collective-permute-start | bytes 196616 | tf_op jit(solution)/shard_map/ppermute | solution.py:154
  76.1 0.9 collective-permute-done.theirs_ref
  77.0 0.7 gram.1
  77.7 11.6 %all_to_all.27 = f32[16,40,128]{2,1,0:T(8,128)S(1)} all-to-all(f32[16,40,128]{2,1,0:T(8,128)S(1)} %bitcast.12), channel_id=1, replica_groups=mesh['rows_0'=8,'rows_1'=4,'rows_2'=4,'cols'=2] {'rows_1','rows_2'}, dimensions={0} | all-to-all | bytes 655360 | tf_op jit(solution)/shard_map/all_to_all | solution.py:318
  89.3 10.4 %all_to_all.28 = f32[8,40,128]{2,1,0:T(8,128)S(1)} all-to-all(f32[8,40,128]{2,1,0:T(8,128)S(1)} %broadcast_in_dim.4), channel_id=1, replica_groups=mesh['rows_0'=8,'rows_1'=4,'rows_2'=4,'cols'=2] {'rows_0'}, dimensions={0} | all-to-all | bytes 327680 | tf_op jit(solution)/shard_map/all_to_all | solution.py:150
  99.8 11.0 %all_to_all.29 = f32[16,40,128]{2,1,0:T(8,128)S(1)} all-to-all(f32[16,40,128]{2,1,0:T(8,128)S(1)} %broadcast_in_dim.5), channel_id=1, replica_groups=mesh['rows_0'=8,'rows_1'=4,'rows_2'=4,'cols'=2] {'rows_1','rows_2'}, dimensions={0} | all-to-all | bytes 655360 | tf_op jit(solution)/shard_map/all_to_all | solution.py:150
  110.8 3.9 %collective-permute-start.1 = (f32[640,128]{1,0:T(8,128)S(1)}, f32[640,128]{1,0:T(8,128)S(1)}, u32[]{:S(2)}, u32[]{:S(2)}) collective-permute-start(f32[640,128]{1,0:T(8,128)S(1)} %bitcast.10), channel_id=1, source_target_pairs={{0,1},{1,0},{2,3},{3,2},{4,5},{5,4},{6,7},{7,6},{8,9},{9,8},{10,11... | collective-permute-start | bytes 983048 | tf_op jit(solution)/shard_map/ppermute | solution.py:154
  114.7 1.3 collective-permute-done.1.theirs_ref
  116.0 14.9 %cholesky.1 = f32[512,256]{1,0:T(8,128)} custom-call(s32[1]{0:T(128)} %bitcast.column_ref, f32[640,128]{1,0:T(8,128)S(1)} %bitcast.11, f32[640,128]{1,0:T(8,128)S(1)} %collective-permute-done.1.theirs_ref), custom_call_target="tpu_custom_call" | custom-call | tf_op jit(solution)/shard_map/cholesky/pallas_call | solution.py:322
  (4 shorter events, 0.1 us)
Async XLA Ops:
  5.8 45.0 %copy-start = (s32[8192]{0:T(1024)S(1)}, s32[8192]{0:T(1024)}, u32[]{:S(2)}) copy-start(s32[8192]{0:T(1024)} %kept_scalar_ref.1) | copy-start | bytes 98308
  73.3 3.7 %collective-permute-start = (f32[128,128]{1,0:T(8,128)S(1)}, f32[128,128]{1,0:T(8,128)S(1)}, u32[]{:S(2)}, u32[]{:S(2)}) collective-permute-start(f32[128,128]{1,0:T(8,128)S(1)} %bitcast.14), channel_id=1, source_target_pairs={{0,1},{1,0},{2,3},{3,2},{4,5},{5,4},{6,7},{7,6},{8,9},{9,8},{10,11... | collective-permute-start | bytes 196616 | tf_op jit(solution)/shard_map/ppermute | solution.py:154
  110.8 5.2 %collective-permute-start.1 = (f32[640,128]{1,0:T(8,128)S(1)}, f32[640,128]{1,0:T(8,128)S(1)}, u32[]{:S(2)}, u32[]{:S(2)}) collective-permute-start(f32[640,128]{1,0:T(8,128)S(1)} %bitcast.10), channel_id=1, source_target_pairs={{0,1},{1,0},{2,3},{3,2},{4,5},{5,4},{6,7},{7,6},{8,9},{9,8},{10,11... | collective-permute-start | bytes 983048 | tf_op jit(solution)/shard_map/ppermute | solution.py:154

commit v4 on v3

--- a/solution.py
+++ b/solution.py
@@ -115,35 +115,52 @@
         return carry
 
     lax.fori_loop(0, 64, rest, 0)
-    left = lax.broadcasted_iota(jnp.int32, (64, 128), 1) < 64
-    a, b = first[...] * scale, second[...] * scale
-    out_ref[pl.ds(0, 64, stride=2), :] = jnp.where(left, a, pltpu.roll(b, 64, 1))
-    out_ref[pl.ds(1, 64, stride=2), :] = jnp.where(left, pltpu.roll(a, 64, 1), b)
-
-
-def gram_kernel(scale, column_ref, mine_ref, theirs_ref, sketch_ref, out_ref):
-    turned, theirs = mine_ref[...].T, theirs_ref[...].T
-    own = [turned[:64], turned[64:]]
-    other = [theirs[:64], theirs[64:]]
-    sketch_ref[:, :128] = own[0]
-    sketch_ref[:, 128:] = own[1]
-    zero = column_ref[0] == 0
+    left = lax.broadcasted_iota(jnp.int32, (8, 128), 1) < 64
+    for h, chosen in enumerate((first, second)):
+        for i in range(4):
+            x = chosen[16 * i : 16 * i + 8] * scale
+            y = chosen[16 * i + 8 : 16 * i + 16] * scale
+            even = jnp.where(left, x, pltpu.roll(y, 64, 1))
+            odd = jnp.where(left, pltpu.roll(x, 64, 1), y)
+            for z in range(8):
+                out_ref[pl.ds(z * 128 + h * 4 + i, 8, stride=16), :] = even
+                out_ref[pl.ds(z * 128 + 8 + h * 4 + i, 8, stride=16), :] = odd
+
+
+def gram_product(a, b):
+    ah, am, al = thirds(a)
+    bh, bm, bl = thirds(b)
+    top = jnp.concatenate([bh, bm], 1)
+
+    def dot(x, y):
+        return lax.dot_general(x, y, (((1,), (1,)), ((), ())), preferred_element_type=jnp.float32)
+
+    small = dot(jnp.concatenate([ah, al], 1), jnp.concatenate([bl, bh], 1))
+    small = small + dot(jnp.concatenate([am, am], 1), top)
+    return small + dot(jnp.concatenate([ah, ah], 1), top)
+
+
+def gram_kernel(scale, column_ref, z_ref, mine_ref, theirs_ref, sketch_ref, out_ref, turned):
+    zero, z = column_ref[0] == 0, z_ref[0]
+    for h in range(2):
+        turned[...] = mine_ref[pl.ds(h * 4 + z // 2, 128, stride=8), :].T
+        sketch_ref[:, h * 128 : h * 128 + 128] = turned[pl.ds(pl.multiple_of(z % 2 * 64, 64), 64), :]
+
+    def wide(ref, h):
+        return jnp.concatenate([ref[pl.ds(h * 4 + i, 128, stride=8), :] for i in range(4)], 1)
 
     def choose(a, b):
         return jnp.where(zero, a, b)
 
-    left = choose(own[0], other[1])
-    pairs = [
-        (own[0], own[0]),
-        (own[0], own[1]),
-        (own[1], own[1]),
-        (left, choose(other[0], own[0])),
-        (left, choose(other[1], own[1])),
-    ]
-    for index, (a, b) in enumerate(pairs):
-        out_ref[index * 128 : (index + 1) * 128, :] = scale * lax.dot_general(
-            a, b, (((0,), (0,)), ((), ())), precision=lax.Precision.HIGHEST, preferred_element_type=jnp.float32
-        )
+    own = [wide(mine_ref, 0), wide(mine_ref, 1)]
+    other = [wide(theirs_ref, 0), wide(theirs_ref, 1)]
+    both = jnp.concatenate(own, 0)
+    square = gram_product(both, both) * scale
+    right = jnp.concatenate([choose(other[0], own[0]), choose(other[1], own[1])], 0)
+    cross = gram_product(choose(own[0], other[1]), right) * scale
+    blocks = [square[:128, :128], square[:128, 128:], square[128:, 128:], cross[:, :128], cross[:, 128:]]
+    for index, block in enumerate(blocks):
+        out_ref[index * 128 : (index + 1) * 128, :] = block
 
 
 def copies(shard, axes, count):
@@ -288,13 +305,13 @@
         in_specs=[pl.BlockSpec(memory_space=pltpu.HBM), VMEM],
         out_specs=VMEM,
         scratch_shapes=[pltpu.VMEM((1024, 256), f32), pltpu.SemaphoreType.DMA((8,))],
-        compiler_params=pltpu.CompilerParams(vmem_limit_bytes=60 * 1024 * 1024),
+        compiler_params=pltpu.CompilerParams(vmem_limit_bytes=52 * 1024 * 1024 + 256 * 1024),
         name="local_transform",
     )(design, signs.reshape(8, 128))
     columns = lax.all_to_all(local.reshape(128, 16, 128), ROWS, 0, 0, tiled=True)
     entries = pl.pallas_call(
         functools.partial(select_kernel, 1.0 / math.sqrt(131072)),
-        out_shape=jax.ShapeDtypeStruct((128, 128), f32),
+        out_shape=jax.ShapeDtypeStruct((1024, 128), f32),
         in_specs=[VMEM, VMEM, SMEM],
         out_specs=VMEM,
         scratch_shapes=[
@@ -305,18 +322,17 @@
         compiler_params=LIMIT,
         name="select",
     )(columns, kept.reshape(64, 128), kept)
-    entries = lax.all_to_all(entries.reshape(128, 1, 128), ROWS, 0, 0, tiled=True)
-    entries = entries.reshape(128, 128)
+    entries = lax.all_to_all(entries.reshape(128, 8, 128), ROWS, 0, 0, tiled=True).reshape(1024, 128)
     sketch, partial = pl.pallas_call(
         functools.partial(gram_kernel, 1.0 / 8192),
         out_shape=(jax.ShapeDtypeStruct((64, 256), f32), jax.ShapeDtypeStruct((640, 128), f32)),
-        in_specs=[SMEM, VMEM, VMEM],
+        in_specs=[SMEM, SMEM, VMEM, VMEM],
         out_specs=(VMEM, VMEM),
+        scratch_shapes=[pltpu.VMEM((128, 128), f32)],
         compiler_params=LIMIT,
         name="gram",
-    )(column.reshape(1), entries, swap_cores(entries))
+    )(column.reshape(1), lax.axis_index("rows_0").reshape(1), entries, swap_cores(entries))
     share = jnp.sum(lax.all_to_all(partial.reshape(16, 40, 128), PLANE, 0, 0, tiled=True), axis=0)
-    share = jnp.sum(copies(share, "rows_0", 8), axis=0)
     mine = copies(share, PLANE, 16).reshape(640, 128)
     theirs = swap_cores(mine)
     factor = pl.pallas_call(

time: 131 us -> 128 us (0.977)
  blocking collectives: 96.6 us -> 92.8 us
    all_to_all x2 -> x1, blocking collectives: 21.4 us -> 11 us  [copies(): lax.all_to_all(jnp.broadcast_to(shard[None], (count, *shard.shape)), axes...]
    all_to_all x1, blocking collectives: 18.6 us -> 25.5 us  [body(): lax.all_to_all(entries.reshape(128, 8, 128), ROWS, 0, 0, tiled=True)]
    pallas_call x1, Pallas kernels: 5.15 us -> 3.48 us  [body(): pl.pallas_call(local_kernel, out_shape=jax.ShapeDtypeStruct((2048, 128),...]
where the time goes in v4:
time: 128 us; the launch traced here: 127 us
  blocking collectives  92.8 us (72%)
  Pallas kernels  24.2 us (19%)
  starting transfers between devices  6.2 us (5%)
  waiting for transfers between devices  2.79 us (2%)
    all_to_all x1, blocking collectives, body(): lax.all_to_all(local.reshape(128, 16, 128), ROWS, 0, 0, tiled=True)  44.7 us
    all_to_all x1, blocking collectives, body(): lax.all_to_all(entries.reshape(128, 8, 128), ROWS, 0, 0, tiled=True)  25.5 us
    pallas_call x1, Pallas kernels, body(): pl.pallas_call(cholesky_kernel, out_shape=jax.ShapeDtypeStruct((512, 256)...  14.9 us
    all_to_all x1, blocking collectives, body(): lax.all_to_all(partial.reshape(16, 40, 128), PLANE, 0, 0, tiled=True)  11.6 us
    all_to_all x1, blocking collectives, copies(): lax.all_to_all(jnp.broadcast_to(shard[None], (count, *shard.shape)), axes...  11 us
    ppermute x2, starting transfers between devices, swap_cores(): return lax.ppermute(value, 'cols', [(0, 1), (1, 0)])  6.2 us
    pallas_call x1, Pallas kernels, body(): pl.pallas_call(functools.partial(select_kernel, 1.0 / math.sqrt(131072)),...  4.17 us
    pallas_call x1, Pallas kernels, body(): pl.pallas_call(local_kernel, out_shape=jax.ShapeDtypeStruct((2048, 128),...  3.48 us
  transfers between devices with their start and end apart: 2, of which 2 were waited for; matrix products, arithmetic and copies ran while one was open for 0% of the time, Pallas kernels for 0%

profile of v4, /device:TPU:1, one launch (start us, length us, event | category | flops | bytes accessed | tf_op | source)
XLA Modules:
  0.0 127.5 jit_solution(12316179119624117421)
XLA Ops:
  0.6 0.0 copy-start.1
  0.6 0.7 copy-done.1
  1.3 3.5 %local_transform.1 = f32[2048,128]{1,0:T(8,128)S(1)} custom-call(f32[1024,256]{1,0:T(8,128)} %design_ref.1, s32[8,128]{1,0:T(8,128)S(1)} %bitcast.17), custom_call_target="tpu_custom_call" | custom-call | tf_op jit(solution)/shard_map/local_transform/pallas_call | solution.py:302
  4.8 0.0 copy-start
  4.8 44.7 %all_to_all.20.columns_ref = f32[128,16,128]{2,1,0:T(8,128)S(1)} all-to-all(f32[128,16,128]{2,1,0:T(8,128)S(1)} %bitcast.9), channel_id=1, replica_groups=mesh['rows_0'=8,'rows_1'=4,'rows_2'=4,'cols'=2] {'rows_0','rows_1','rows..., dimensions={0} | all-to-all | bytes 2097152 | tf_op jit(solution)/shard_map/all_to_all | solution.py:311
  49.6 0.0 copy-done
  49.6 4.2 %select.1 = f32[1024,128]{1,0:T(8,128)S(1)} custom-call(f32[128,16,128]{2,1,0:T(8,128)S(1)} %all_to_all.20.columns_ref, s32[64,128]{1,0:T(8,128)S(1)} %bitcast.16, s32[8192]{0:T(1024)S(1)} %copy-done), custom_call_target="tpu_custom_call" | custom-call | tf_op jit(solution)/shard_map/select/pallas_call | solution.py:312
  53.7 25.5 %all_to_all.21 = f32[128,8,128]{2,1,0:T(8,128)S(1)} all-to-all(f32[128,8,128]{2,1,0:T(8,128)S(1)} %bitcast.10), channel_id=1, replica_groups=mesh['rows_0'=8,'rows_1'=4,'rows_2'=4,'cols'=2] {'rows_0','rows_1','rows..., dimensions={0} | all-to-all | bytes 1048576 | tf_op jit(solution)/shard_map/all_to_all | solution.py:325
  79.3 3.9 %collective-permute-start = (f32[1024,128]{1,0:T(8,128)S(1)}, f32[1024,128]{1,0:T(8,128)S(1)}, u32[]{:S(2)}, u32[]{:S(2)}) collective-permute-start(f32[1024,128]{1,0:T(8,128)S(1)} %bitcast.11), channel_id=1, source_target_pairs={{0,1},{1,0},{2,3},{3,2},{4,5},{5,4},{6,7},{7,6},{8,9},{9,8},{10,11... | collective-permute-start | bytes 1572872 | tf_op jit(solution)/shard_map/ppermute | solution.py:171
  83.2 1.5 %collective-permute-done.theirs_ref = f32[1024,128]{1,0:T(8,128)S(1)} collective-permute-done((f32[1024,128]{1,0:T(8,128)S(1)}, f32[1024,128]{1,0:T(8,128)S(1)}, u32[]{:S(2)}, u32[]{:S(2)}) %collective-permute-start) | collective-permute-done | bytes 524320 | tf_op jit(solution)/shard_map/ppermute | solution.py:171
  84.7 1.7 %gram.1 = (f32[64,256]{1,0:T(8,128)}, f32[640,128]{1,0:T(8,128)S(1)}) custom-call(s32[1]{0:T(128)} %bitcast.column_ref, s32[1]{0:T(128)} %bitcast.1.z_ref, f32[1024,128]{1,0:T(8,128)S(1)} %bitcast.12, f32[1024,128]{1,0:T(8,128)S(1)} %collective-permute-done.theirs_ref), custom_call_target="tpu_custom_call" | custom-call | tf_op jit(solution)/shard_map/gram/pallas_call | solution.py:326
  86.5 11.6 %all_to_all.22 = f32[16,40,128]{2,1,0:T(8,128)S(1)} all-to-all(f32[16,40,128]{2,1,0:T(8,128)S(1)} %bitcast.15), channel_id=1, replica_groups=mesh['rows_0'=8,'rows_1'=4,'rows_2'=4,'cols'=2] {'rows_1','rows_2'}, dimensions={0} | all-to-all | bytes 655360 | tf_op jit(solution)/shard_map/all_to_all | solution.py:335
  98.1 11.0 %all_to_all.23 = f32[16,40,128]{2,1,0:T(8,128)S(1)} all-to-all(f32[16,40,128]{2,1,0:T(8,128)S(1)} %broadcast_in_dim.2), channel_id=1, replica_groups=mesh['rows_0'=8,'rows_1'=4,'rows_2'=4,'cols'=2] {'rows_1','rows_2'}, dimensions={0} | all-to-all | bytes 655360 | tf_op jit(solution)/shard_map/all_to_all | solution.py:167
  109.1 2.3 %collective-permute-start.1 = (f32[640,128]{1,0:T(8,128)S(1)}, f32[640,128]{1,0:T(8,128)S(1)}, u32[]{:S(2)}, u32[]{:S(2)}) collective-permute-start(f32[640,128]{1,0:T(8,128)S(1)} %bitcast.13), channel_id=1, source_target_pairs={{0,1},{1,0},{2,3},{3,2},{4,5},{5,4},{6,7},{7,6},{8,9},{9,8},{10,11... | collective-permute-start | bytes 983048 | tf_op jit(solution)/shard_map/ppermute | solution.py:171
  111.3 1.3 collective-permute-done.1.theirs_ref
  112.6 14.9 %cholesky.1 = f32[512,256]{1,0:T(8,128)} custom-call(s32[1]{0:T(128)} %bitcast.column_ref, f32[640,128]{1,0:T(8,128)S(1)} %bitcast.14, f32[640,128]{1,0:T(8,128)S(1)} %collective-permute-done.1.theirs_ref), custom_call_target="tpu_custom_call" | custom-call | tf_op jit(solution)/shard_map/cholesky/pallas_call | solution.py:338
  (2 shorter events, 0.0 us)
Async XLA Ops:
  0.6 0.7 copy-start.1
  4.8 44.8 %copy-start = (s32[8192]{0:T(1024)S(1)}, s32[8192]{0:T(1024)}, u32[]{:S(2)}) copy-start(s32[8192]{0:T(1024)} %kept_scalar_ref.1) | copy-start | bytes 98308
  79.3 5.5 %collective-permute-start = (f32[1024,128]{1,0:T(8,128)S(1)}, f32[1024,128]{1,0:T(8,128)S(1)}, u32[]{:S(2)}, u32[]{:S(2)}) collective-permute-start(f32[1024,128]{1,0:T(8,128)S(1)} %bitcast.11), channel_id=1, source_target_pairs={{0,1},{1,0},{2,3},{3,2},{4,5},{5,4},{6,7},{7,6},{8,9},{9,8},{10,11... | collective-permute-start | bytes 1572872 | tf_op jit(solution)/shard_map/ppermute | solution.py:171
  109.1 3.5 %collective-permute-start.1 = (f32[640,128]{1,0:T(8,128)S(1)}, f32[640,128]{1,0:T(8,128)S(1)}, u32[]{:S(2)}, u32[]{:S(2)}) collective-permute-start(f32[640,128]{1,0:T(8,128)S(1)} %bitcast.13), channel_id=1, source_target_pairs={{0,1},{1,0},{2,3},{3,2},{4,5},{5,4},{6,7},{7,6},{8,9},{9,8},{10,11... | collective-permute-start | bytes 983048 | tf_op jit(solution)/shard_map/ppermute | solution.py:171

commit v5 on v4

--- a/solution.py
+++ b/solution.py
@@ -39,27 +39,18 @@
     return (1 - 2 * (parity & 1)).astype(jnp.float32).astype(jnp.bfloat16)
 
 
-def local_kernel(design_ref, signs_ref, out_ref, held, sems):
-    def fetch(b):
-        rows = pl.ds(b * 128, 128)
-        return pltpu.make_async_copy(design_ref.at[rows, :], held.at[rows, :], sems.at[b])
-
-    for b in range(8):
-        fetch(b).start()
+def local_kernel(design_ref, signs_ref, out_ref):
     table = sylvester(128)
-    parts = [[], []]
-    for b in range(8):
-        fetch(b).wait()
-        sign = signs_ref[b : b + 1, :].astype(jnp.float32)
-        for half in range(2):
-            piece = held[b * 128 : (b + 1) * 128, half * 128 : (half + 1) * 128].T * sign
-            high, middle, low = thirds(piece)
+    for half in range(2):
+        parts = []
+        for b in range(8):
+            piece = design_ref[b * 128 : (b + 1) * 128, half * 128 : (half + 1) * 128].T
+            high, middle, low = thirds(piece * signs_ref[b : b + 1, :])
             total = jnp.dot(low, table, preferred_element_type=jnp.float32)
             total += jnp.dot(middle, table, preferred_element_type=jnp.float32)
             total += jnp.dot(high, table, preferred_element_type=jnp.float32)
-            parts[half].append(total)
-    for half in range(2):
-        for q, mixed in enumerate(butterflies(parts[half])):
+            parts.append(total)
+        for q, mixed in enumerate(butterflies(parts)):
             out_ref[pl.ds(half * 8 + q, 128, stride=16), :] = mixed
 
 
@@ -87,7 +78,17 @@
 
     zero = jnp.zeros((8, 128), jnp.float32)
 
+    def merged(values):
+        for bit in (1, 2, 4):
+            low = (sublane & bit) == 0
+            values = [
+                jnp.where(low, x, y) + pltpu.roll(jnp.where(low, y, x), 8 - bit, 0)
+                for x, y in zip(values[::2], values[1::2])
+            ]
+        return values[0]
+
     def group(step, carry):
+        sums = [[], []]
         for inner in range(8):
             chunk = step * 8 + inner
             start = kept_scalar_ref[chunk * 128] >> 10
@@ -95,8 +96,11 @@
             so_far = (zero, zero)
             for w in range(WINDOW):
                 so_far = picked(jnp.minimum(start + w, 127), lane, key, so_far)
-            first[pl.ds(chunk, 1), :] = jnp.sum(so_far[0], axis=0, keepdims=True)
-            second[pl.ds(chunk, 1), :] = jnp.sum(so_far[1], axis=0, keepdims=True)
+            sums[0].append(so_far[0])
+            sums[1].append(so_far[1])
+        rows = pl.ds(pl.multiple_of(step * 8, 8), 8)
+        first[rows, :] = merged(sums[0])
+        second[rows, :] = merged(sums[1])
         return carry
 
     lax.fori_loop(0, 8, group, 0)
@@ -140,27 +144,34 @@
     return small + dot(jnp.concatenate([ah, ah], 1), top)
 
 
-def gram_kernel(scale, column_ref, z_ref, mine_ref, theirs_ref, sketch_ref, out_ref, turned):
-    zero, z = column_ref[0] == 0, z_ref[0]
+def wide(ref, h):
+    return jnp.concatenate([ref[pl.ds(h * 4 + i, 128, stride=8), :] for i in range(4)], 1)
+
+
+def own_kernel(scale, z_ref, mine_ref, sketch_ref, out_ref, turned):
+    z = z_ref[0]
     for h in range(2):
         turned[...] = mine_ref[pl.ds(h * 4 + z // 2, 128, stride=8), :].T
         sketch_ref[:, h * 128 : h * 128 + 128] = turned[pl.ds(pl.multiple_of(z % 2 * 64, 64), 64), :]
-
-    def wide(ref, h):
-        return jnp.concatenate([ref[pl.ds(h * 4 + i, 128, stride=8), :] for i in range(4)], 1)
+    both = jnp.concatenate([wide(mine_ref, 0), wide(mine_ref, 1)], 0)
+    square = gram_product(both, both) * scale
+    for index, block in enumerate([square[:128, :128], square[:128, 128:], square[128:, 128:]]):
+        out_ref[index * 128 : (index + 1) * 128, :] = block
+
+
+def cross_kernel(scale, column_ref, mine_ref, theirs_ref, blocks_ref, out_ref):
+    zero = column_ref[0] == 0
 
     def choose(a, b):
         return jnp.where(zero, a, b)
 
     own = [wide(mine_ref, 0), wide(mine_ref, 1)]
     other = [wide(theirs_ref, 0), wide(theirs_ref, 1)]
-    both = jnp.concatenate(own, 0)
-    square = gram_product(both, both) * scale
     right = jnp.concatenate([choose(other[0], own[0]), choose(other[1], own[1])], 0)
     cross = gram_product(choose(own[0], other[1]), right) * scale
-    blocks = [square[:128, :128], square[:128, 128:], square[128:, 128:], cross[:, :128], cross[:, 128:]]
-    for index, block in enumerate(blocks):
-        out_ref[index * 128 : (index + 1) * 128, :] = block
+    out_ref[:384, :] = blocks_ref[...]
+    out_ref[384:512, :] = cross[:, :128]
+    out_ref[512:, :] = cross[:, 128:]
 
 
 def copies(shard, axes, count):
@@ -302,12 +313,11 @@
     local = pl.pallas_call(
         local_kernel,
         out_shape=jax.ShapeDtypeStruct((2048, 128), f32),
-        in_specs=[pl.BlockSpec(memory_space=pltpu.HBM), VMEM],
+        in_specs=[VMEM, VMEM],
         out_specs=VMEM,
-        scratch_shapes=[pltpu.VMEM((1024, 256), f32), pltpu.SemaphoreType.DMA((8,))],
-        compiler_params=pltpu.CompilerParams(vmem_limit_bytes=52 * 1024 * 1024 + 256 * 1024),
+        compiler_params=LIMIT,
         name="local_transform",
-    )(design, signs.reshape(8, 128))
+    )(design, signs.astype(f32).reshape(8, 128))
     columns = lax.all_to_all(local.reshape(128, 16, 128), ROWS, 0, 0, tiled=True)
     entries = pl.pallas_call(
         functools.partial(select_kernel, 1.0 / math.sqrt(131072)),
@@ -323,15 +333,25 @@
         name="select",
     )(columns, kept.reshape(64, 128), kept)
     entries = lax.all_to_all(entries.reshape(128, 8, 128), ROWS, 0, 0, tiled=True).reshape(1024, 128)
-    sketch, partial = pl.pallas_call(
-        functools.partial(gram_kernel, 1.0 / 8192),
-        out_shape=(jax.ShapeDtypeStruct((64, 256), f32), jax.ShapeDtypeStruct((640, 128), f32)),
-        in_specs=[SMEM, SMEM, VMEM, VMEM],
+    theirs = swap_cores(entries)
+    sketch, blocks = pl.pallas_call(
+        functools.partial(own_kernel, 1.0 / 8192),
+        out_shape=(jax.ShapeDtypeStruct((64, 256), f32), jax.ShapeDtypeStruct((384, 128), f32)),
+        in_specs=[SMEM, VMEM],
         out_specs=(VMEM, VMEM),
         scratch_shapes=[pltpu.VMEM((128, 128), f32)],
         compiler_params=LIMIT,
-        name="gram",
-    )(column.reshape(1), lax.axis_index("rows_0").reshape(1), entries, swap_cores(entries))
+        cost_estimate=pl.CostEstimate(flops=800_000_000, bytes_accessed=1_000_000, transcendentals=0),
+        name="own_gram",
+    )(lax.axis_index("rows_0").reshape(1), entries)
+    partial = pl.pallas_call(
+        functools.partial(cross_kernel, 1.0 / 8192),
+        out_shape=jax.ShapeDtypeStruct((640, 128), f32),
+        in_specs=[SMEM, VMEM, VMEM, VMEM],
+        out_specs=VMEM,
+        compiler_params=LIMIT,
+        name="cross_gram",
+    )(column.reshape(1), entries, theirs, blocks)
     share = jnp.sum(lax.all_to_all(partial.reshape(16, 40, 128), PLANE, 0, 0, tiled=True), axis=0)
     mine = copies(share, PLANE, 16).reshape(640, 128)
     theirs = swap_cores(mine)

time: 128 us -> 126 us (0.984)
  Pallas kernels: 24.2 us -> 22 us
    pallas_call x1, Pallas kernels: 3.48 us -> 0.94 us  [body(): pl.pallas_call(local_kernel, out_shape=jax.ShapeDtypeStruct((2048, 128),...]
  transfers between devices with their start and end apart: 2 -> 2, of which waited for: 2 -> 2; matrix products, arithmetic and copies ran while one was open for 0% -> 0% of each run, Pallas kernels for 0% -> 1%
where the time goes in v5:
time: 126 us; the launch traced here: 125 us
  blocking collectives  92.8 us (74%)
  Pallas kernels  22 us (17%)
  starting transfers between devices  6.2 us (5%)
  waiting for transfers between devices  1.59 us (1%)
    all_to_all x1, blocking collectives, body(): lax.all_to_all(local.reshape(128, 16, 128), ROWS, 0, 0, tiled=True)  44.8 us
    all_to_all x1, blocking collectives, body(): lax.all_to_all(entries.reshape(128, 8, 128), ROWS, 0, 0, tiled=True)  25.5 us
    pallas_call x1, Pallas kernels, body(): pl.pallas_call(cholesky_kernel, out_shape=jax.ShapeDtypeStruct((512, 256)...  14.9 us
    all_to_all x1, blocking collectives, body(): lax.all_to_all(partial.reshape(16, 40, 128), PLANE, 0, 0, tiled=True)  11.6 us
    all_to_all x1, blocking collectives, copies(): lax.all_to_all(jnp.broadcast_to(shard[None], (count, *shard.shape)), axes...  11 us
    ppermute x2, starting transfers between devices, swap_cores(): return lax.ppermute(value, 'cols', [(0, 1), (1, 0)])  6.2 us
    pallas_call x1, Pallas kernels, body(): pl.pallas_call(functools.partial(select_kernel, 1.0 / math.sqrt(131072)),...  4.22 us
  transfers between devices with their start and end apart: 2, of which 2 were waited for; matrix products, arithmetic and copies ran while one was open for 0% of the time, Pallas kernels for 1%

profile of v5, /device:TPU:1, one launch (start us, length us, event | category | flops | bytes accessed | tf_op | source)
XLA Modules:
  0.0 125.2 jit_solution(18356816484067136882)
XLA Ops:
  0.6 0.7 convert_bitcast_fusion.signs_ref
  1.3 0.0 copy-start
  1.3 1.2 copy-done
  2.5 0.9 local_transform.1
  3.5 0.0 copy-start.1
  3.5 44.8 %all_to_all.20.columns_ref = f32[128,16,128]{2,1,0:T(8,128)S(1)} all-to-all(f32[128,16,128]{2,1,0:T(8,128)S(1)} %bitcast.10), channel_id=1, replica_groups=mesh['rows_0'=8,'rows_1'=4,'rows_2'=4,'cols'=2] {'rows_0','rows_1','rows..., dimensions={0} | all-to-all | bytes 2097152 | tf_op jit(solution)/shard_map/all_to_all | solution.py:321
  48.3 0.0 copy-done.1
  48.3 4.2 %select.1 = f32[1024,128]{1,0:T(8,128)S(1)} custom-call(f32[128,16,128]{2,1,0:T(8,128)S(1)} %all_to_all.20.columns_ref, s32[64,128]{1,0:T(8,128)S(1)} %bitcast.18, s32[8192]{0:T(1024)S(1)} %copy-done.1), custom_call_target="tpu_custom_call" | custom-call | tf_op jit(solution)/shard_map/select/pallas_call | solution.py:322
  52.5 25.5 %all_to_all.21 = f32[128,8,128]{2,1,0:T(8,128)S(1)} all-to-all(f32[128,8,128]{2,1,0:T(8,128)S(1)} %bitcast.11), channel_id=1, replica_groups=mesh['rows_0'=8,'rows_1'=4,'rows_2'=4,'cols'=2] {'rows_0','rows_1','rows..., dimensions={0} | all-to-all | bytes 1048576 | tf_op jit(solution)/shard_map/all_to_all | solution.py:335
  78.0 3.9 %collective-permute-start = (f32[1024,128]{1,0:T(8,128)S(1)}, f32[1024,128]{1,0:T(8,128)S(1)}, u32[]{:S(2)}, u32[]{:S(2)}) collective-permute-start(f32[1024,128]{1,0:T(8,128)S(1)} %bitcast.12), channel_id=1, source_target_pairs={{0,1},{1,0},{2,3},{3,2},{4,5},{5,4},{6,7},{7,6},{8,9},{9,8},{10,11... | collective-permute-start | bytes 1572872 | tf_op jit(solution)/shard_map/ppermute | solution.py:182
  82.0 1.2 own_gram.1
  83.2 0.3 collective-permute-done.theirs_ref
  83.5 0.7 cross_gram.1
  84.2 11.6 %all_to_all.22 = f32[16,40,128]{2,1,0:T(8,128)S(1)} all-to-all(f32[16,40,128]{2,1,0:T(8,128)S(1)} %bitcast.17), channel_id=1, replica_groups=mesh['rows_0'=8,'rows_1'=4,'rows_2'=4,'cols'=2] {'rows_1','rows_2'}, dimensions={0} | all-to-all | bytes 655360 | tf_op jit(solution)/shard_map/all_to_all | solution.py:355
  95.8 11.0 %all_to_all.23 = f32[16,40,128]{2,1,0:T(8,128)S(1)} all-to-all(f32[16,40,128]{2,1,0:T(8,128)S(1)} %broadcast_in_dim.2), channel_id=1, replica_groups=mesh['rows_0'=8,'rows_1'=4,'rows_2'=4,'cols'=2] {'rows_1','rows_2'}, dimensions={0} | all-to-all | bytes 655360 | tf_op jit(solution)/shard_map/all_to_all | solution.py:178
  106.8 2.3 %collective-permute-start.1 = (f32[640,128]{1,0:T(8,128)S(1)}, f32[640,128]{1,0:T(8,128)S(1)}, u32[]{:S(2)}, u32[]{:S(2)}) collective-permute-start(f32[640,128]{1,0:T(8,128)S(1)} %bitcast.15), channel_id=1, source_target_pairs={{0,1},{1,0},{2,3},{3,2},{4,5},{5,4},{6,7},{7,6},{8,9},{9,8},{10,11... | collective-permute-start | bytes 983048 | tf_op jit(solution)/shard_map/ppermute | solution.py:182
  109.1 1.3 %collective-permute-done.1.theirs_ref = f32[640,128]{1,0:T(8,128)S(1)} collective-permute-done((f32[640,128]{1,0:T(8,128)S(1)}, f32[640,128]{1,0:T(8,128)S(1)}, u32[]{:S(2)}, u32[]{:S(2)}) %collective-permute-start.1) | collective-permute-done | bytes 327712 | tf_op jit(solution)/shard_map/ppermute | solution.py:182
  110.4 14.9 %cholesky.1 = f32[512,256]{1,0:T(8,128)} custom-call(s32[1]{0:T(128)} %bitcast.6.column_ref, f32[640,128]{1,0:T(8,128)S(1)} %bitcast.16, f32[640,128]{1,0:T(8,128)S(1)} %collective-permute-done.1.theirs_ref), custom_call_target="tpu_custom_call" | custom-call | tf_op jit(solution)/shard_map/cholesky/pallas_call | solution.py:358
  (2 shorter events, 0.0 us)
Async XLA Ops:
  1.3 1.2 copy-start
  3.5 44.8 %copy-start.1 = (s32[8192]{0:T(1024)S(1)}, s32[8192]{0:T(1024)}, u32[]{:S(2)}) copy-start(s32[8192]{0:T(1024)} %kept_scalar_ref.1) | copy-start | bytes 98308
  78.0 5.5 %collective-permute-start = (f32[1024,128]{1,0:T(8,128)S(1)}, f32[1024,128]{1,0:T(8,128)S(1)}, u32[]{:S(2)}, u32[]{:S(2)}) collective-permute-start(f32[1024,128]{1,0:T(8,128)S(1)} %bitcast.12), channel_id=1, source_target_pairs={{0,1},{1,0},{2,3},{3,2},{4,5},{5,4},{6,7},{7,6},{8,9},{9,8},{10,11... | collective-permute-start | bytes 1572872 | tf_op jit(solution)/shard_map/ppermute | solution.py:182
  106.8 3.5 %collective-permute-start.1 = (f32[640,128]{1,0:T(8,128)S(1)}, f32[640,128]{1,0:T(8,128)S(1)}, u32[]{:S(2)}, u32[]{:S(2)}) collective-permute-start(f32[640,128]{1,0:T(8,128)S(1)} %bitcast.15), channel_id=1, source_target_pairs={{0,1},{1,0},{2,3},{3,2},{4,5},{5,4},{6,7},{7,6},{8,9},{9,8},{10,11... | collective-permute-start | bytes 983048 | tf_op jit(solution)/shard_map/ppermute | solution.py:182

commit v6 on v5

--- a/solution.py
+++ b/solution.py
@@ -15,7 +15,7 @@
 SMEM = pl.BlockSpec(memory_space=pltpu.SMEM)
 LIMIT = pltpu.CompilerParams(vmem_limit_bytes=32 * 1024 * 1024)
 WINDOW = 4
-GROUP = 1
+GROUP = 2
 AHEAD = 2
 
 
@@ -54,7 +54,9 @@
             out_ref[pl.ds(half * 8 + q, 128, stride=16), :] = mixed
 
 
-def select_kernel(scale, columns_ref, kept_ref, kept_scalar_ref, out_ref, work, first, second):
+def select_kernel(scale, columns_ref, kept_ref, kept_any_ref, out_ref, work, first, second, kept_scalar_ref, sem):
+    fetch = pltpu.make_async_copy(kept_any_ref, kept_scalar_ref, sem)
+    fetch.start()
     for low in range(16):
         mixed = butterflies(columns_ref[high * 16 + low] for high in range(8))
         for high in range(8):
@@ -63,6 +65,7 @@
         mixed = butterflies(work[high * 16 + low] for low in range(16))
         for low in range(16):
             work[high * 16 + low] = mixed[low]
+    fetch.wait()
     sublane = lax.broadcasted_iota(jnp.int32, (8, 128), 0)
 
     def picked(block, lane, key, so_far):
@@ -87,11 +90,12 @@
             ]
         return values[0]
 
-    def group(step, carry):
+    def group(step, widest):
         sums = [[], []]
         for inner in range(8):
             chunk = step * 8 + inner
             start = kept_scalar_ref[chunk * 128] >> 10
+            widest = jnp.maximum(widest, (kept_scalar_ref[chunk * 128 + 127] >> 10) - start)
             lane, key = ids(chunk)
             so_far = (zero, zero)
             for w in range(WINDOW):
@@ -101,9 +105,9 @@
         rows = pl.ds(pl.multiple_of(step * 8, 8), 8)
         first[rows, :] = merged(sums[0])
         second[rows, :] = merged(sums[1])
-        return carry
-
-    lax.fori_loop(0, 8, group, 0)
+        return widest
+
+    widest = lax.fori_loop(0, 8, group, 0, unroll=True)
 
     def rest(chunk, carry):
         start = (kept_scalar_ref[chunk * 128] >> 10) + WINDOW
@@ -118,7 +122,10 @@
 
         return carry
 
-    lax.fori_loop(0, 64, rest, 0)
+    @pl.when(widest >= WINDOW)
+    def _():
+        lax.fori_loop(0, 64, rest, 0)
+
     left = lax.broadcasted_iota(jnp.int32, (8, 128), 1) < 64
     for h, chosen in enumerate((first, second)):
         for i in range(4):
@@ -229,37 +236,33 @@
             entries[8 * k : 8 * k + 8] = spread(here[:, base + k : base + k + 1])
         e = [[entries[pl.ds(8 * k + i, 8, stride=0), :] if k >= i else None for k in range(8)] for i in range(8)]
         m = [jnp.where(inside, jnp.where(lanes == base + k, 1.0, 0.0), rows[pl.ds(k, 8, stride=0), :]) for k in range(8)]
-        d, u, r = [None] * 8, [[None] * 8 for _ in range(8)], [None] * 8
+        end = (s // GROUP + 1) * GROUP
+        near = range(s + 1, min(end + AHEAD, 16))
+        total = {t: jnp.where(inside, 0.0, strips[t]) for t in near}
+        c = {t: [spread(strips[t][:, base + k : base + k + 1]) for k in range(8)] for t in near}
+        below = lanes < base + 8
         for k in range(8):
-            d[k] = lax.rsqrt(e[k][k])
-            for j in range(k + 1, 8):
-                u[k][j] = e[k][j] * d[k]
-            r[k] = m[k] * d[k]
+            d = lax.rsqrt(e[k][k])
+            u = [e[k][j] * d if j > k else None for j in range(8)]
             for i in range(k + 1, 8):
                 for j in range(i, 8):
-                    e[i][j] = e[i][j] - u[k][i] * u[k][j]
+                    e[i][j] = e[i][j] - u[i] * u[j]
+            r = m[k] * d
             for i in range(k + 1, 8):
-                m[i] = m[i] - u[k][i] * r[k]
-        z = [None] * 8
-        for k in reversed(range(8)):
-            z[k] = r[k] * d[k]
-            for j in reversed(range(k + 1, 8)):
-                z[k] = z[k] - (u[k][j] * d[k]) * z[j]
-        end = (s // GROUP + 1) * GROUP
-        for t in range(s + 1, min(end + AHEAD, 16)):
-            there = strips[t]
-            total = jnp.where(inside, 0.0, there)
-            for k in range(8):
-                total = total - spread(there[:, base + k : base + k + 1]) * z[k]
-            strips[t] = total
-        for k in range(8):
-            row = r[k]
-            inverse_ref[base + k : base + k + 1, :] = jnp.where(lanes < base + 8, row, 0.0)[:1]
-            row = jnp.where(lanes < base + 8, 0.0, row)
-            row = jnp.where(lanes == base + k, e[k][k] * d[k], row)
+                m[i] = m[i] - u[i] * r
+            for t in near:
+                scaled = c[t][k] * d
+                for i in range(k + 1, 8):
+                    c[t][i] = c[t][i] - u[i] * scaled
+                total[t] = total[t] - scaled * r
+            inverse_ref[base + k : base + k + 1, :] = jnp.where(below, r, 0.0)[:1]
+            row = jnp.where(below, 0.0, r)
+            row = jnp.where(lanes == base + k, e[k][k] * d, row)
             for j in range(k + 1, 8):
-                row = jnp.where(lanes == base + j, u[k][j], row)
+                row = jnp.where(lanes == base + j, u[j], row)
             upper_ref[base + k : base + k + 1, :] = row[:1]
+        for t in near:
+            strips[t] = total[t]
         if later:
             later.pop(0)()
         if s + 1 == end and end + AHEAD < 16:
@@ -322,12 +325,14 @@
     entries = pl.pallas_call(
         functools.partial(select_kernel, 1.0 / math.sqrt(131072)),
         out_shape=jax.ShapeDtypeStruct((1024, 128), f32),
-        in_specs=[VMEM, VMEM, SMEM],
+        in_specs=[VMEM, VMEM, pl.BlockSpec(memory_space=pl.ANY)],
         out_specs=VMEM,
         scratch_shapes=[
             pltpu.VMEM((128, 16, 128), f32),
             pltpu.VMEM((64, 128), f32),
             pltpu.VMEM((64, 128), f32),
+            pltpu.SMEM((8192,), jnp.int32),
+            pltpu.SemaphoreType.DMA(()),
         ],
         compiler_params=LIMIT,
         name="select",

time: 126 us -> 123 us (0.976)
  Pallas kernels: 22 us -> 19 us
    pallas_call x1, Pallas kernels: 4.22 us -> 2.24 us  [body(): pl.pallas_call(functools.partial(select_kernel, 1.0 / math.sqrt(131072)),...]
where the time goes in v6:
time: 123 us; the launch traced here: 122 us
  blocking collectives  92.9 us (76%)
  Pallas kernels  19 us (15%)
  starting transfers between devices  6.19 us (5%)
  waiting for transfers between devices  1.6 us (1%)
  local copies, waits for them, and re-layouts  1.25 us (1%)
    all_to_all x1, blocking collectives, body(): lax.all_to_all(local.reshape(128, 16, 128), ROWS, 0, 0, tiled=True)  44.8 us
    all_to_all x1, blocking collectives, body(): lax.all_to_all(entries.reshape(128, 8, 128), ROWS, 0, 0, tiled=True)  25.5 us
    pallas_call x1, Pallas kernels, body(): pl.pallas_call(cholesky_kernel, out_shape=jax.ShapeDtypeStruct((512, 256)...  13.9 us
    all_to_all x1, blocking collectives, body(): lax.all_to_all(partial.reshape(16, 40, 128), PLANE, 0, 0, tiled=True)  11.6 us
    all_to_all x1, blocking collectives, copies(): lax.all_to_all(jnp.broadcast_to(shard[None], (count, *shard.shape)), axes...  11 us
    ppermute x2, starting transfers between devices, swap_cores(): return lax.ppermute(value, 'cols', [(0, 1), (1, 0)])  6.19 us
  transfers between devices with their start and end apart: 2, of which 2 were waited for; matrix products, arithmetic and copies ran while one was open for 0% of the time, Pallas kernels for 1%

profile of v6, /device:TPU:1, one launch (start us, length us, event | category | flops | bytes accessed | tf_op | source)
XLA Modules:
  0.0 122.3 jit_solution(16997054794866035512)
XLA Ops:
  0.6 0.7 convert_bitcast_fusion.signs_ref
  1.3 0.0 copy-start
  1.3 1.2 copy-done
  2.5 0.9 local_transform.1
  3.5 0.0 copy-start.1
  3.5 44.8 %all_to_all.20.columns_ref = f32[128,16,128]{2,1,0:T(8,128)S(1)} all-to-all(f32[128,16,128]{2,1,0:T(8,128)S(1)} %bitcast.10), channel_id=1, replica_groups=mesh['rows_0'=8,'rows_1'=4,'rows_2'=4,'cols'=2] {'rows_0','rows_1','rows..., dimensions={0} | all-to-all | bytes 2097152 | tf_op jit(solution)/shard_map/all_to_all | solution.py:324
  48.3 0.0 copy-done.1
  48.3 2.2 %select.1 = f32[1024,128]{1,0:T(8,128)S(1)} custom-call(f32[128,16,128]{2,1,0:T(8,128)S(1)} %all_to_all.20.columns_ref, s32[64,128]{1,0:T(8,128)S(1)} %bitcast.18, s32[8192]{0:T(1024)S(1)} %copy-done.1), custom_call_target="tpu_custom_call" | custom-call | tf_op jit(solution)/shard_map/select/pallas_call | solution.py:325
  50.5 25.5 %all_to_all.21 = f32[128,8,128]{2,1,0:T(8,128)S(1)} all-to-all(f32[128,8,128]{2,1,0:T(8,128)S(1)} %bitcast.11), channel_id=1, replica_groups=mesh['rows_0'=8,'rows_1'=4,'rows_2'=4,'cols'=2] {'rows_0','rows_1','rows..., dimensions={0} | all-to-all | bytes 1048576 | tf_op jit(solution)/shard_map/all_to_all | solution.py:340
  76.0 3.9 %collective-permute-start = (f32[1024,128]{1,0:T(8,128)S(1)}, f32[1024,128]{1,0:T(8,128)S(1)}, u32[]{:S(2)}, u32[]{:S(2)}) collective-permute-start(f32[1024,128]{1,0:T(8,128)S(1)} %bitcast.12), channel_id=1, source_target_pairs={{0,1},{1,0},{2,3},{3,2},{4,5},{5,4},{6,7},{7,6},{8,9},{9,8},{10,11... | collective-permute-start | bytes 1572872 | tf_op jit(solution)/shard_map/ppermute | solution.py:189
  80.0 1.2 own_gram.1
  81.2 0.3 collective-permute-done.theirs_ref
  81.5 0.7 cross_gram.1
  82.2 11.6 %all_to_all.22 = f32[16,40,128]{2,1,0:T(8,128)S(1)} all-to-all(f32[16,40,128]{2,1,0:T(8,128)S(1)} %bitcast.17), channel_id=1, replica_groups=mesh['rows_0'=8,'rows_1'=4,'rows_2'=4,'cols'=2] {'rows_1','rows_2'}, dimensions={0} | all-to-all | bytes 655360 | tf_op jit(solution)/shard_map/all_to_all | solution.py:360
  93.9 11.0 %all_to_all.23 = f32[16,40,128]{2,1,0:T(8,128)S(1)} all-to-all(f32[16,40,128]{2,1,0:T(8,128)S(1)} %broadcast_in_dim.2), channel_id=1, replica_groups=mesh['rows_0'=8,'rows_1'=4,'rows_2'=4,'cols'=2] {'rows_1','rows_2'}, dimensions={0} | all-to-all | bytes 655360 | tf_op jit(solution)/shard_map/all_to_all | solution.py:185
  104.9 2.3 %collective-permute-start.1 = (f32[640,128]{1,0:T(8,128)S(1)}, f32[640,128]{1,0:T(8,128)S(1)}, u32[]{:S(2)}, u32[]{:S(2)}) collective-permute-start(f32[640,128]{1,0:T(8,128)S(1)} %bitcast.15), channel_id=1, source_target_pairs={{0,1},{1,0},{2,3},{3,2},{4,5},{5,4},{6,7},{7,6},{8,9},{9,8},{10,11... | collective-permute-start | bytes 983048 | tf_op jit(solution)/shard_map/ppermute | solution.py:189
  107.1 1.3 %collective-permute-done.1.theirs_ref = f32[640,128]{1,0:T(8,128)S(1)} collective-permute-done((f32[640,128]{1,0:T(8,128)S(1)}, f32[640,128]{1,0:T(8,128)S(1)}, u32[]{:S(2)}, u32[]{:S(2)}) %collective-permute-start.1) | collective-permute-done | bytes 327712 | tf_op jit(solution)/shard_map/ppermute | solution.py:189
  108.4 13.9 %cholesky.1 = f32[512,256]{1,0:T(8,128)} custom-call(s32[1]{0:T(128)} %bitcast.6.column_ref, f32[640,128]{1,0:T(8,128)S(1)} %bitcast.16, f32[640,128]{1,0:T(8,128)S(1)} %collective-permute-done.1.theirs_ref), custom_call_target="tpu_custom_call" | custom-call | tf_op jit(solution)/shard_map/cholesky/pallas_call | solution.py:363
  (2 shorter events, 0.0 us)
Async XLA Ops:
  1.3 1.2 %copy-start = (f32[1024,256]{1,0:T(8,128)S(1)}, f32[1024,256]{1,0:T(8,128)}, u32[]{:S(2)}) copy-start(f32[1024,256]{1,0:T(8,128)} %design_ref.1) | copy-start | bytes 3145732
  3.5 44.8 %copy-start.1 = (s32[8192]{0:T(1024)S(1)}, s32[8192]{0:T(1024)}, u32[]{:S(2)}) copy-start(s32[8192]{0:T(1024)} %kept_any_ref.1) | copy-start | bytes 98308
  76.0 5.5 %collective-permute-start = (f32[1024,128]{1,0:T(8,128)S(1)}, f32[1024,128]{1,0:T(8,128)S(1)}, u32[]{:S(2)}, u32[]{:S(2)}) collective-permute-start(f32[1024,128]{1,0:T(8,128)S(1)} %bitcast.12), channel_id=1, source_target_pairs={{0,1},{1,0},{2,3},{3,2},{4,5},{5,4},{6,7},{7,6},{8,9},{9,8},{10,11... | collective-permute-start | bytes 1572872 | tf_op jit(solution)/shard_map/ppermute | solution.py:189
  104.9 3.5 %collective-permute-start.1 = (f32[640,128]{1,0:T(8,128)S(1)}, f32[640,128]{1,0:T(8,128)S(1)}, u32[]{:S(2)}, u32[]{:S(2)}) collective-permute-start(f32[640,128]{1,0:T(8,128)S(1)} %bitcast.15), channel_id=1, source_target_pairs={{0,1},{1,0},{2,3},{3,2},{4,5},{5,4},{6,7},{7,6},{8,9},{9,8},{10,11... | collective-permute-start | bytes 983048 | tf_op jit(solution)/shard_map/ppermute | solution.py:189

commit v7 on v6

--- a/solution.py
+++ b/solution.py
@@ -11,6 +11,7 @@
 
 ROWS = ("rows_0", "rows_1", "rows_2")
 PLANE = ("rows_1", "rows_2")
+Z_FASTEST = ("rows_1", "rows_2", "rows_0")
 VMEM = pl.BlockSpec(memory_space=pltpu.VMEM)
 SMEM = pl.BlockSpec(memory_space=pltpu.SMEM)
 LIMIT = pltpu.CompilerParams(vmem_limit_bytes=32 * 1024 * 1024)
@@ -58,7 +59,7 @@
     fetch = pltpu.make_async_copy(kept_any_ref, kept_scalar_ref, sem)
     fetch.start()
     for low in range(16):
-        mixed = butterflies(columns_ref[high * 16 + low] for high in range(8))
+        mixed = butterflies(columns_ref[low * 8 + high] for high in range(8))
         for high in range(8):
             work[high * 16 + low] = mixed[high]
     for high in range(8):
@@ -134,8 +135,8 @@
             even = jnp.where(left, x, pltpu.roll(y, 64, 1))
             odd = jnp.where(left, pltpu.roll(x, 64, 1), y)
             for z in range(8):
-                out_ref[pl.ds(z * 128 + h * 4 + i, 8, stride=16), :] = even
-                out_ref[pl.ds(z * 128 + 8 + h * 4 + i, 8, stride=16), :] = odd
+                out_ref[pl.ds(z * 8 + h * 4 + i, 8, stride=128), :] = even
+                out_ref[pl.ds(64 + z * 8 + h * 4 + i, 8, stride=128), :] = odd
 
 
 def gram_product(a, b):
@@ -321,7 +322,7 @@
         compiler_params=LIMIT,
         name="local_transform",
     )(design, signs.astype(f32).reshape(8, 128))
-    columns = lax.all_to_all(local.reshape(128, 16, 128), ROWS, 0, 0, tiled=True)
+    columns = lax.all_to_all(local.reshape(128, 16, 128), Z_FASTEST, 0, 0, tiled=True)
     entries = pl.pallas_call(
         functools.partial(select_kernel, 1.0 / math.sqrt(131072)),
         out_shape=jax.ShapeDtypeStruct((1024, 128), f32),
@@ -337,7 +338,7 @@
         compiler_params=LIMIT,
         name="select",
     )(columns, kept.reshape(64, 128), kept)
-    entries = lax.all_to_all(entries.reshape(128, 8, 128), ROWS, 0, 0, tiled=True).reshape(1024, 128)
+    entries = lax.all_to_all(entries.reshape(128, 8, 128), Z_FASTEST, 0, 0, tiled=True).reshape(1024, 128)
     theirs = swap_cores(entries)
     sketch, blocks = pl.pallas_call(
         functools.partial(own_kernel, 1.0 / 8192),

time: 123 us -> 122 us (level)
  no operation moved by 1% of the time
where the time goes in v7:
time: 122 us
  blocking collectives  91.8 us (75%)
  Pallas kernels  19.1 us (16%)
  starting transfers between devices  6.65 us (5%)
  waiting for transfers between devices  1.61 us (1%)
  local copies, waits for them, and re-layouts  1.25 us (1%)
    all_to_all x1, blocking collectives, body(): lax.all_to_all(local.reshape(128, 16, 128), Z_FASTEST, 0, 0, tiled=True)  46.4 us
    all_to_all x1, blocking collectives, body(): lax.all_to_all(entries.reshape(128, 8, 128), Z_FASTEST, 0, 0, tiled=True)  22.8 us
    pallas_call x1, Pallas kernels, body(): pl.pallas_call(cholesky_kernel, out_shape=jax.ShapeDtypeStruct((512, 256)...  14 us
    all_to_all x1, blocking collectives, body(): lax.all_to_all(partial.reshape(16, 40, 128), PLANE, 0, 0, tiled=True)  11.6 us
    all_to_all x1, blocking collectives, copies(): lax.all_to_all(jnp.broadcast_to(shard[None], (count, *shard.shape)), axes...  11 us
    ppermute x2, starting transfers between devices, swap_cores(): return lax.ppermute(value, 'cols', [(0, 1), (1, 0)])  6.65 us
  transfers between devices with their start and end apart: 2, of which 2 were waited for; matrix products, arithmetic and copies ran while one was open for 0% of the time, Pallas kernels for 1%

profile of v7, /device:TPU:1, one launch (start us, length us, event | category | flops | bytes accessed | tf_op | source)
XLA Modules:
  0.0 121.8 jit_solution(4916237502877156755)
XLA Ops:
  0.6 0.7 convert_bitcast_fusion.signs_ref
  1.3 0.0 copy-start
  1.3 1.2 %copy-done = f32[1024,256]{1,0:T(8,128)S(1)} copy-done((f32[1024,256]{1,0:T(8,128)S(1)}, f32[1024,256]{1,0:T(8,128)}, u32[]{:S(2)}) %copy-start) | copy-done | bytes 1048600
  2.5 0.9 local_transform.1
  3.5 0.0 copy-start.1
  3.5 46.4 %all_to_all.20.columns_ref = f32[128,16,128]{2,1,0:T(8,128)S(1)} all-to-all(f32[128,16,128]{2,1,0:T(8,128)S(1)} %bitcast.10), channel_id=1, replica_groups=mesh['rows_0'=8,'rows_1'=4,'rows_2'=4,'cols'=2] {'rows_1','rows_2','rows..., dimensions={0} | all-to-all | bytes 2097152 | tf_op jit(solution)/shard_map/all_to_all | solution.py:325
  49.9 0.0 copy-done.1
  49.9 2.3 %select.1 = f32[1024,128]{1,0:T(8,128)S(1)} custom-call(f32[128,16,128]{2,1,0:T(8,128)S(1)} %all_to_all.20.columns_ref, s32[64,128]{1,0:T(8,128)S(1)} %bitcast.18, s32[8192]{0:T(1024)S(1)} %copy-done.1), custom_call_target="tpu_custom_call" | custom-call | tf_op jit(solution)/shard_map/select/pallas_call | solution.py:326
  52.2 22.8 %all_to_all.21 = f32[128,8,128]{2,1,0:T(8,128)S(1)} all-to-all(f32[128,8,128]{2,1,0:T(8,128)S(1)} %bitcast.11), channel_id=1, replica_groups=mesh['rows_0'=8,'rows_1'=4,'rows_2'=4,'cols'=2] {'rows_1','rows_2','rows..., dimensions={0} | all-to-all | bytes 1048576 | tf_op jit(solution)/shard_map/all_to_all | solution.py:341
  75.0 4.4 %collective-permute-start = (f32[1024,128]{1,0:T(8,128)S(1)}, f32[1024,128]{1,0:T(8,128)S(1)}, u32[]{:S(2)}, u32[]{:S(2)}) collective-permute-start(f32[1024,128]{1,0:T(8,128)S(1)} %bitcast.12), channel_id=1, source_target_pairs={{0,1},{1,0},{2,3},{3,2},{4,5},{5,4},{6,7},{7,6},{8,9},{9,8},{10,11... | collective-permute-start | bytes 1572872 | tf_op jit(solution)/shard_map/ppermute | solution.py:190
  79.4 1.2 own_gram.1
  80.6 0.4 collective-permute-done.theirs_ref
  80.9 0.7 cross_gram.1
  81.6 11.6 %all_to_all.22 = f32[16,40,128]{2,1,0:T(8,128)S(1)} all-to-all(f32[16,40,128]{2,1,0:T(8,128)S(1)} %bitcast.17), channel_id=1, replica_groups=mesh['rows_0'=8,'rows_1'=4,'rows_2'=4,'cols'=2] {'rows_1','rows_2'}, dimensions={0} | all-to-all | bytes 655360 | tf_op jit(solution)/shard_map/all_to_all | solution.py:361
  93.3 11.0 %all_to_all.23 = f32[16,40,128]{2,1,0:T(8,128)S(1)} all-to-all(f32[16,40,128]{2,1,0:T(8,128)S(1)} %broadcast_in_dim.2), channel_id=1, replica_groups=mesh['rows_0'=8,'rows_1'=4,'rows_2'=4,'cols'=2] {'rows_1','rows_2'}, dimensions={0} | all-to-all | bytes 655360 | tf_op jit(solution)/shard_map/all_to_all | solution.py:186
  104.3 2.3 %collective-permute-start.1 = (f32[640,128]{1,0:T(8,128)S(1)}, f32[640,128]{1,0:T(8,128)S(1)}, u32[]{:S(2)}, u32[]{:S(2)}) collective-permute-start(f32[640,128]{1,0:T(8,128)S(1)} %bitcast.15), channel_id=1, source_target_pairs={{0,1},{1,0},{2,3},{3,2},{4,5},{5,4},{6,7},{7,6},{8,9},{9,8},{10,11... | collective-permute-start | bytes 983048 | tf_op jit(solution)/shard_map/ppermute | solution.py:190
  106.5 1.3 %collective-permute-done.1.theirs_ref = f32[640,128]{1,0:T(8,128)S(1)} collective-permute-done((f32[640,128]{1,0:T(8,128)S(1)}, f32[640,128]{1,0:T(8,128)S(1)}, u32[]{:S(2)}, u32[]{:S(2)}) %collective-permute-start.1) | collective-permute-done | bytes 327712 | tf_op jit(solution)/shard_map/ppermute | solution.py:190
  107.8 14.0 %cholesky.1 = f32[512,256]{1,0:T(8,128)} custom-call(s32[1]{0:T(128)} %bitcast.6.column_ref, f32[640,128]{1,0:T(8,128)S(1)} %bitcast.16, f32[640,128]{1,0:T(8,128)S(1)} %collective-permute-done.1.theirs_ref), custom_call_target="tpu_custom_call" | custom-call | tf_op jit(solution)/shard_map/cholesky/pallas_call | solution.py:364
  (2 shorter events, 0.0 us)
Async XLA Ops:
  1.3 1.2 %copy-start = (f32[1024,256]{1,0:T(8,128)S(1)}, f32[1024,256]{1,0:T(8,128)}, u32[]{:S(2)}) copy-start(f32[1024,256]{1,0:T(8,128)} %design_ref.1) | copy-start | bytes 3145732
  3.5 46.4 %copy-start.1 = (s32[8192]{0:T(1024)S(1)}, s32[8192]{0:T(1024)}, u32[]{:S(2)}) copy-start(s32[8192]{0:T(1024)} %kept_any_ref.1) | copy-start | bytes 98308
  75.0 5.9 %collective-permute-start = (f32[1024,128]{1,0:T(8,128)S(1)}, f32[1024,128]{1,0:T(8,128)S(1)}, u32[]{:S(2)}, u32[]{:S(2)}) collective-permute-start(f32[1024,128]{1,0:T(8,128)S(1)} %bitcast.12), channel_id=1, source_target_pairs={{0,1},{1,0},{2,3},{3,2},{4,5},{5,4},{6,7},{7,6},{8,9},{9,8},{10,11... | collective-permute-start | bytes 1572872 | tf_op jit(solution)/shard_map/ppermute | solution.py:190
  104.3 3.5 %collective-permute-start.1 = (f32[640,128]{1,0:T(8,128)S(1)}, f32[640,128]{1,0:T(8,128)S(1)}, u32[]{:S(2)}, u32[]{:S(2)}) collective-permute-start(f32[640,128]{1,0:T(8,128)S(1)} %bitcast.15), channel_id=1, source_target_pairs={{0,1},{1,0},{2,3},{3,2},{4,5},{5,4},{6,7},{7,6},{8,9},{9,8},{10,11... | collective-permute-start | bytes 983048 | tf_op jit(solution)/shard_map/ppermute | solution.py:190

commit v8 on v7

--- a/solution.py
+++ b/solution.py
@@ -276,7 +276,7 @@
                 strips[t] = jnp.where(group, 0.0, strips[t]) - delta[8 * t : 8 * t + 8]
 
 
-def cholesky_kernel(column_ref, mine_ref, theirs_ref, out_ref, gram, upper, inverse, rows_ref, entries_ref):
+def cholesky_kernel(column_ref, mine_ref, theirs_ref, out_ref, gram, upper, inverse, rows_ref, entries_ref, staged, sems):
     zero = column_ref[0] == 0
     names = [(0, 0), (0, 1), (1, 1), (0, 2), (0, 3), (2, 2), (2, 3), (3, 3), (1, 2), (1, 3)]
     place = {name: i for i, name in enumerate(names)}
@@ -291,24 +291,37 @@
     def update(p, i, j):
         gram[place[i, j]] -= product(thirds(upper[p * 4 + i].T), thirds(upper[p * 4 + j]))
 
+    def copy_out(p):
+        rows = pl.ds(p * 128, 128)
+        return pltpu.make_async_copy(staged.at[rows, :], out_ref.at[rows, :], sems.at[p])
+
+    def send(p):
+        for h in range(2):
+            staged[p * 128 : p * 128 + 128, h * 128 : h * 128 + 128] = jnp.where(zero, upper[p * 4 + h], upper[p * 4 + 2 + h])
+        copy_out(p).start()
+
     later = []
     for p in range(4):
         factor_block(gram[place[p, p]], upper.at[p * 4 + p], inverse.at[p], rows_ref, entries_ref, later)
         for work in later:
             work()
         later = []
+        if p in (1, 2):
+            send(p - 1)
         for q in range(p):
             upper[p * 4 + q] = jnp.zeros((128, 128), jnp.float32)
         if p < 3:
             solve(p, p + 1)
             update(p, p + 1, p + 1)
+        if p == 2:
+            send(2)
         for j in range(p + 2, 4):
             later.append(functools.partial(solve, p, j))
             for i in range(p + 1, j + 1):
                 later.append(functools.partial(update, p, i, j))
+    send(3)
     for p in range(4):
-        for h in range(2):
-            out_ref[p * 128 : p * 128 + 128, h * 128 : h * 128 + 128] = jnp.where(zero, upper[p * 4 + h], upper[p * 4 + 2 + h])
+        copy_out(p).wait()
 
 
 def body(design, signs, kept):
@@ -365,13 +378,15 @@
         cholesky_kernel,
         out_shape=jax.ShapeDtypeStruct((512, 256), f32),
         in_specs=[SMEM, VMEM, VMEM],
-        out_specs=VMEM,
+        out_specs=pl.BlockSpec(memory_space=pl.ANY),
         scratch_shapes=[
             pltpu.VMEM((10, 128, 128), f32),
             pltpu.VMEM((16, 128, 128), f32),
             pltpu.VMEM((4, 128, 128), f32),
             pltpu.VMEM((2, 8, 128), f32),
             pltpu.VMEM((2, 64, 128), f32),
+            pltpu.VMEM((512, 256), f32),
+            pltpu.SemaphoreType.DMA((4,)),
         ],
         compiler_params=LIMIT,
         name="cholesky",

time: 122 us -> 122 us (level)
  no operation moved by 1% of the time
where the time goes in v8:
time: 122 us
  blocking collectives  91.8 us (75%)
  Pallas kernels  19 us (16%)
  starting transfers between devices  6.65 us (5%)
  waiting for transfers between devices  1.59 us (1%)
  local copies, waits for them, and re-layouts  1.25 us (1%)
    all_to_all x1, blocking collectives, body(): lax.all_to_all(local.reshape(128, 16, 128), Z_FASTEST, 0, 0, tiled=True)  46.4 us
    all_to_all x1, blocking collectives, body(): lax.all_to_all(entries.reshape(128, 8, 128), Z_FASTEST, 0, 0, tiled=True)  22.8 us
    pallas_call x1, Pallas kernels, body(): pl.pallas_call(cholesky_kernel, out_shape=jax.ShapeDtypeStruct((512, 256)...  13.8 us
    all_to_all x1, blocking collectives, body(): lax.all_to_all(partial.reshape(16, 40, 128), PLANE, 0, 0, tiled=True)  11.6 us
    all_to_all x1, blocking collectives, copies(): lax.all_to_all(jnp.broadcast_to(shard[None], (count, *shard.shape)), axes...  11 us
    ppermute x2, starting transfers between devices, swap_cores(): return lax.ppermute(value, 'cols', [(0, 1), (1, 0)])  6.65 us
  transfers between devices with their start and end apart: 2, of which 2 were waited for; matrix products, arithmetic and copies ran while one was open for 0% of the time, Pallas kernels for 1%

profile of v8, /device:TPU:1, one launch (start us, length us, event | category | flops | bytes accessed | tf_op | source)
XLA Modules:
  0.0 121.8 jit_solution(298367660217044511)
XLA Ops:
  0.6 0.7 convert_bitcast_fusion.signs_ref
  1.3 0.0 copy-start
  1.3 1.2 %copy-done = f32[1024,256]{1,0:T(8,128)S(1)} copy-done((f32[1024,256]{1,0:T(8,128)S(1)}, f32[1024,256]{1,0:T(8,128)}, u32[]{:S(2)}) %copy-start) | copy-done | bytes 1048600
  2.5 0.9 local_transform.1
  3.5 0.0 copy-start.1
  3.5 46.4 %all_to_all.20.columns_ref = f32[128,16,128]{2,1,0:T(8,128)S(1)} all-to-all(f32[128,16,128]{2,1,0:T(8,128)S(1)} %bitcast.10), channel_id=1, replica_groups=mesh['rows_0'=8,'rows_1'=4,'rows_2'=4,'cols'=2] {'rows_1','rows_2','rows..., dimensions={0} | all-to-all | bytes 2097152 | tf_op jit(solution)/shard_map/all_to_all | solution.py:338
  49.9 0.0 copy-done.1
  49.9 2.3 %select.1 = f32[1024,128]{1,0:T(8,128)S(1)} custom-call(f32[128,16,128]{2,1,0:T(8,128)S(1)} %all_to_all.20.columns_ref, s32[64,128]{1,0:T(8,128)S(1)} %bitcast.18, s32[8192]{0:T(1024)S(1)} %copy-done.1), custom_call_target="tpu_custom_call" | custom-call | tf_op jit(solution)/shard_map/select/pallas_call | solution.py:339
  52.2 22.8 %all_to_all.21 = f32[128,8,128]{2,1,0:T(8,128)S(1)} all-to-all(f32[128,8,128]{2,1,0:T(8,128)S(1)} %bitcast.11), channel_id=1, replica_groups=mesh['rows_0'=8,'rows_1'=4,'rows_2'=4,'cols'=2] {'rows_1','rows_2','rows..., dimensions={0} | all-to-all | bytes 1048576 | tf_op jit(solution)/shard_map/all_to_all | solution.py:354
  75.0 4.4 %collective-permute-start = (f32[1024,128]{1,0:T(8,128)S(1)}, f32[1024,128]{1,0:T(8,128)S(1)}, u32[]{:S(2)}, u32[]{:S(2)}) collective-permute-start(f32[1024,128]{1,0:T(8,128)S(1)} %bitcast.12), channel_id=1, source_target_pairs={{0,1},{1,0},{2,3},{3,2},{4,5},{5,4},{6,7},{7,6},{8,9},{9,8},{10,11... | collective-permute-start | bytes 1572872 | tf_op jit(solution)/shard_map/ppermute | solution.py:190
  79.4 1.2 own_gram.1
  80.6 0.3 collective-permute-done.theirs_ref
  80.9 0.7 cross_gram.1
  81.6 11.6 %all_to_all.22 = f32[16,40,128]{2,1,0:T(8,128)S(1)} all-to-all(f32[16,40,128]{2,1,0:T(8,128)S(1)} %bitcast.17), channel_id=1, replica_groups=mesh['rows_0'=8,'rows_1'=4,'rows_2'=4,'cols'=2] {'rows_1','rows_2'}, dimensions={0} | all-to-all | bytes 655360 | tf_op jit(solution)/shard_map/all_to_all | solution.py:374
  93.3 11.0 %all_to_all.23 = f32[16,40,128]{2,1,0:T(8,128)S(1)} all-to-all(f32[16,40,128]{2,1,0:T(8,128)S(1)} %broadcast_in_dim.2), channel_id=1, replica_groups=mesh['rows_0'=8,'rows_1'=4,'rows_2'=4,'cols'=2] {'rows_1','rows_2'}, dimensions={0} | all-to-all | bytes 655360 | tf_op jit(solution)/shard_map/all_to_all | solution.py:186
  104.3 2.3 %collective-permute-start.1 = (f32[640,128]{1,0:T(8,128)S(1)}, f32[640,128]{1,0:T(8,128)S(1)}, u32[]{:S(2)}, u32[]{:S(2)}) collective-permute-start(f32[640,128]{1,0:T(8,128)S(1)} %bitcast.15), channel_id=1, source_target_pairs={{0,1},{1,0},{2,3},{3,2},{4,5},{5,4},{6,7},{7,6},{8,9},{9,8},{10,11... | collective-permute-start | bytes 983048 | tf_op jit(solution)/shard_map/ppermute | solution.py:190
  106.5 1.3 %collective-permute-done.1.theirs_ref = f32[640,128]{1,0:T(8,128)S(1)} collective-permute-done((f32[640,128]{1,0:T(8,128)S(1)}, f32[640,128]{1,0:T(8,128)S(1)}, u32[]{:S(2)}, u32[]{:S(2)}) %collective-permute-start.1) | collective-permute-done | bytes 327712 | tf_op jit(solution)/shard_map/ppermute | solution.py:190
  107.8 13.8 %cholesky.1 = f32[512,256]{1,0:T(8,128)} custom-call(s32[1]{0:T(128)} %bitcast.6.column_ref, f32[640,128]{1,0:T(8,128)S(1)} %bitcast.16, f32[640,128]{1,0:T(8,128)S(1)} %collective-permute-done.1.theirs_ref), custom_call_target="tpu_custom_call" | custom-call | tf_op jit(solution)/shard_map/cholesky/pallas_call | solution.py:377
  (2 shorter events, 0.0 us)
Async XLA Ops:
  1.3 1.2 %copy-start = (f32[1024,256]{1,0:T(8,128)S(1)}, f32[1024,256]{1,0:T(8,128)}, u32[]{:S(2)}) copy-start(f32[1024,256]{1,0:T(8,128)} %design_ref.1) | copy-start | bytes 3145732
  3.5 46.4 %copy-start.1 = (s32[8192]{0:T(1024)S(1)}, s32[8192]{0:T(1024)}, u32[]{:S(2)}) copy-start(s32[8192]{0:T(1024)} %kept_any_ref.1) | copy-start | bytes 98308
  75.0 5.9 %collective-permute-start = (f32[1024,128]{1,0:T(8,128)S(1)}, f32[1024,128]{1,0:T(8,128)S(1)}, u32[]{:S(2)}, u32[]{:S(2)}) collective-permute-start(f32[1024,128]{1,0:T(8,128)S(1)} %bitcast.12), channel_id=1, source_target_pairs={{0,1},{1,0},{2,3},{3,2},{4,5},{5,4},{6,7},{7,6},{8,9},{9,8},{10,11... | collective-permute-start | bytes 1572872 | tf_op jit(solution)/shard_map/ppermute | solution.py:190
  104.3 3.5 %collective-permute-start.1 = (f32[640,128]{1,0:T(8,128)S(1)}, f32[640,128]{1,0:T(8,128)S(1)}, u32[]{:S(2)}, u32[]{:S(2)}) collective-permute-start(f32[640,128]{1,0:T(8,128)S(1)} %bitcast.15), channel_id=1, source_target_pairs={{0,1},{1,0},{2,3},{3,2},{4,5},{5,4},{6,7},{7,6},{8,9},{9,8},{10,11... | collective-permute-start | bytes 983048 | tf_op jit(solution)/shard_map/ppermute | solution.py:190

commit v9 on v8

--- a/solution.py
+++ b/solution.py
@@ -42,14 +42,14 @@
 
 def local_kernel(design_ref, signs_ref, out_ref):
     table = sylvester(128)
+    twice = jnp.concatenate([table, table], 0)
     for half in range(2):
         parts = []
         for b in range(8):
             piece = design_ref[b * 128 : (b + 1) * 128, half * 128 : (half + 1) * 128].T
             high, middle, low = thirds(piece * signs_ref[b : b + 1, :])
             total = jnp.dot(low, table, preferred_element_type=jnp.float32)
-            total += jnp.dot(middle, table, preferred_element_type=jnp.float32)
-            total += jnp.dot(high, table, preferred_element_type=jnp.float32)
+            total += jnp.dot(jnp.concatenate([high, middle], 1), twice, preferred_element_type=jnp.float32)
             parts.append(total)
         for q, mixed in enumerate(butterflies(parts)):
             out_ref[pl.ds(half * 8 + q, 128, stride=16), :] = mixed

time: 122 us -> 122 us (level)
  no operation moved by 1% of the time
where the time goes in v9:
time: 122 us
  blocking collectives  91.8 us (75%)
  Pallas kernels  18.9 us (15%)
  starting transfers between devices  6.66 us (5%)
  waiting for transfers between devices  1.59 us (1%)
  local copies, waits for them, and re-layouts  1.25 us (1%)
    all_to_all x1, blocking collectives, body(): lax.all_to_all(local.reshape(128, 16, 128), Z_FASTEST, 0, 0, tiled=True)  46.4 us
    all_to_all x1, blocking collectives, body(): lax.all_to_all(entries.reshape(128, 8, 128), Z_FASTEST, 0, 0, tiled=True)  22.8 us
    pallas_call x1, Pallas kernels, body(): pl.pallas_call(cholesky_kernel, out_shape=jax.ShapeDtypeStruct((512, 256)...  13.8 us
    all_to_all x1, blocking collectives, body(): lax.all_to_all(partial.reshape(16, 40, 128), PLANE, 0, 0, tiled=True)  11.6 us
    all_to_all x1, blocking collectives, copies(): lax.all_to_all(jnp.broadcast_to(shard[None], (count, *shard.shape)), axes...  11 us
    ppermute x2, starting transfers between devices, swap_cores(): return lax.ppermute(value, 'cols', [(0, 1), (1, 0)])  6.66 us
  transfers between devices with their start and end apart: 2, of which 2 were waited for; matrix products, arithmetic and copies ran while one was open for 0% of the time, Pallas kernels for 1%

profile of v9, /device:TPU:1, one launch (start us, length us, event | category | flops | bytes accessed | tf_op | source)
XLA Modules:
  0.0 121.8 jit_solution(2305608806968874215)
XLA Ops:
  0.6 0.7 convert_bitcast_fusion.signs_ref
  1.3 0.0 copy-start
  1.3 1.2 %copy-done = f32[1024,256]{1,0:T(8,128)S(1)} copy-done((f32[1024,256]{1,0:T(8,128)S(1)}, f32[1024,256]{1,0:T(8,128)}, u32[]{:S(2)}) %copy-start) | copy-done | bytes 1048600
  2.5 0.9 local_transform.1
  3.5 0.0 copy-start.1
  3.5 46.4 %all_to_all.20.columns_ref = f32[128,16,128]{2,1,0:T(8,128)S(1)} all-to-all(f32[128,16,128]{2,1,0:T(8,128)S(1)} %bitcast.10), channel_id=1, replica_groups=mesh['rows_0'=8,'rows_1'=4,'rows_2'=4,'cols'=2] {'rows_1','rows_2','rows..., dimensions={0} | all-to-all | bytes 2097152 | tf_op jit(solution)/shard_map/all_to_all | solution.py:338
  49.8 0.0 copy-done.1
  49.8 2.3 %select.1 = f32[1024,128]{1,0:T(8,128)S(1)} custom-call(f32[128,16,128]{2,1,0:T(8,128)S(1)} %all_to_all.20.columns_ref, s32[64,128]{1,0:T(8,128)S(1)} %bitcast.18, s32[8192]{0:T(1024)S(1)} %copy-done.1), custom_call_target="tpu_custom_call" | custom-call | tf_op jit(solution)/shard_map/select/pallas_call | solution.py:339
  52.1 22.8 %all_to_all.21 = f32[128,8,128]{2,1,0:T(8,128)S(1)} all-to-all(f32[128,8,128]{2,1,0:T(8,128)S(1)} %bitcast.11), channel_id=1, replica_groups=mesh['rows_0'=8,'rows_1'=4,'rows_2'=4,'cols'=2] {'rows_1','rows_2','rows..., dimensions={0} | all-to-all | bytes 1048576 | tf_op jit(solution)/shard_map/all_to_all | solution.py:354
  74.9 4.4 %collective-permute-start = (f32[1024,128]{1,0:T(8,128)S(1)}, f32[1024,128]{1,0:T(8,128)S(1)}, u32[]{:S(2)}, u32[]{:S(2)}) collective-permute-start(f32[1024,128]{1,0:T(8,128)S(1)} %bitcast.12), channel_id=1, source_target_pairs={{0,1},{1,0},{2,3},{3,2},{4,5},{5,4},{6,7},{7,6},{8,9},{9,8},{10,11... | collective-permute-start | bytes 1572872 | tf_op jit(solution)/shard_map/ppermute | solution.py:190
  79.3 1.2 own_gram.1
  80.5 0.3 collective-permute-done.theirs_ref
  80.9 0.7 cross_gram.1
  81.6 11.6 %all_to_all.22 = f32[16,40,128]{2,1,0:T(8,128)S(1)} all-to-all(f32[16,40,128]{2,1,0:T(8,128)S(1)} %bitcast.17), channel_id=1, replica_groups=mesh['rows_0'=8,'rows_1'=4,'rows_2'=4,'cols'=2] {'rows_1','rows_2'}, dimensions={0} | all-to-all | bytes 655360 | tf_op jit(solution)/shard_map/all_to_all | solution.py:374
  93.2 11.0 %all_to_all.23 = f32[16,40,128]{2,1,0:T(8,128)S(1)} all-to-all(f32[16,40,128]{2,1,0:T(8,128)S(1)} %broadcast_in_dim.2), channel_id=1, replica_groups=mesh['rows_0'=8,'rows_1'=4,'rows_2'=4,'cols'=2] {'rows_1','rows_2'}, dimensions={0} | all-to-all | bytes 655360 | tf_op jit(solution)/shard_map/all_to_all | solution.py:186
  104.2 2.3 %collective-permute-start.1 = (f32[640,128]{1,0:T(8,128)S(1)}, f32[640,128]{1,0:T(8,128)S(1)}, u32[]{:S(2)}, u32[]{:S(2)}) collective-permute-start(f32[640,128]{1,0:T(8,128)S(1)} %bitcast.15), channel_id=1, source_target_pairs={{0,1},{1,0},{2,3},{3,2},{4,5},{5,4},{6,7},{7,6},{8,9},{9,8},{10,11... | collective-permute-start | bytes 983048 | tf_op jit(solution)/shard_map/ppermute | solution.py:190
  106.5 1.3 %collective-permute-done.1.theirs_ref = f32[640,128]{1,0:T(8,128)S(1)} collective-permute-done((f32[640,128]{1,0:T(8,128)S(1)}, f32[640,128]{1,0:T(8,128)S(1)}, u32[]{:S(2)}, u32[]{:S(2)}) %collective-permute-start.1) | collective-permute-done | bytes 327712 | tf_op jit(solution)/shard_map/ppermute | solution.py:190
  107.7 13.8 %cholesky.1 = f32[512,256]{1,0:T(8,128)} custom-call(s32[1]{0:T(128)} %bitcast.6.column_ref, f32[640,128]{1,0:T(8,128)S(1)} %bitcast.16, f32[640,128]{1,0:T(8,128)S(1)} %collective-permute-done.1.theirs_ref), custom_call_target="tpu_custom_call" | custom-call | tf_op jit(solution)/shard_map/cholesky/pallas_call | solution.py:377
  (2 shorter events, 0.0 us)
Async XLA Ops:
  1.3 1.2 %copy-start = (f32[1024,256]{1,0:T(8,128)S(1)}, f32[1024,256]{1,0:T(8,128)}, u32[]{:S(2)}) copy-start(f32[1024,256]{1,0:T(8,128)} %design_ref.1) | copy-start | bytes 3145732
  3.5 46.4 %copy-start.1 = (s32[8192]{0:T(1024)S(1)}, s32[8192]{0:T(1024)}, u32[]{:S(2)}) copy-start(s32[8192]{0:T(1024)} %kept_any_ref.1) | copy-start | bytes 98308
  74.9 5.9 %collective-permute-start = (f32[1024,128]{1,0:T(8,128)S(1)}, f32[1024,128]{1,0:T(8,128)S(1)}, u32[]{:S(2)}, u32[]{:S(2)}) collective-permute-start(f32[1024,128]{1,0:T(8,128)S(1)} %bitcast.12), channel_id=1, source_target_pairs={{0,1},{1,0},{2,3},{3,2},{4,5},{5,4},{6,7},{7,6},{8,9},{9,8},{10,11... | collective-permute-start | bytes 1572872 | tf_op jit(solution)/shard_map/ppermute | solution.py:190
  104.2 3.5 %collective-permute-start.1 = (f32[640,128]{1,0:T(8,128)S(1)}, f32[640,128]{1,0:T(8,128)S(1)}, u32[]{:S(2)}, u32[]{:S(2)}) collective-permute-start(f32[640,128]{1,0:T(8,128)S(1)} %bitcast.15), channel_id=1, source_target_pairs={{0,1},{1,0},{2,3},{3,2},{4,5},{5,4},{6,7},{7,6},{8,9},{9,8},{10,11... | collective-permute-start | bytes 983048 | tf_op jit(solution)/shard_map/ppermute | solution.py:190
